TPU v7x, 32 devices: a whole 2x2x4 slice. The times are simulated.
32 devices in a mesh: freq: 2 (over x), tile: 16 (over z, y, core).
Axes of the slice: x: 2, y: 2, z: 4, core: 2. Of those that a mesh axis runs over, the one named last changes fastest.
Arguments:
- left_basis: bfloat16 [4, 8192, 2, 1536], P('freq', 'tile'), may hold values from -0.078125 to 0.078125
- right_basis: bfloat16 [4, 8192, 2, 1536], P('freq', 'tile'), may hold values from -0.25 to 0.25
- start_model: float32 [4, 8192, 128], P('freq', 'tile'), may hold values from -3 to 3
- recorded: float32 [4, 8192, 128], P('freq', 'tile'), may hold values from -6 to 6
- tile_ranks: int32 [16, 16], replicated, may hold values from 16 to 96, as said below
- mute_start: int32 [8192, 64], P('tile'), may hold values from 0 to 127
- thresholds: float32 [64], replicated, may hold values from 0.05 to 0.5
Outputs:
- estimate: float32 [4, 8192, 128], P('freq', 'tile')
- misfit: float32 [4, 8192, 128], P('freq', 'tile')
Inputs may be any that keep to these rules, and one draw needn't show every extreme that they name: `tile_ranks`: some tile has rank 96 and some rank 16.
All inputs are finite; a program needn't handle non-finite values.
Results may differ from a plain program's by a relative error of at most 0.013.
Values may be sent and summed in bfloat16 or wider, within the bound.
No kernel may reach another device: no remote copies, remote signals or barrier semaphores. Data moves between devices by JAX's collectives and lax.ppermute only.
A program may use at most 64 MiB of HBM per device.

v0:
```python
import math

import jax
import jax.numpy as jnp
from jax import lax
from jax.experimental import pallas as pl
from jax.experimental.pallas import tpu as pltpu
from jax.sharding import PartitionSpec as P

NT = 256
OUTER = 2
STEP_SIZE = 0.5


def lane_is_real(shape):
    return lax.broadcasted_iota(jnp.int32, shape, 1) < shape[1] // 2


def interleave(vector, scratch):
    rows, columns = vector.shape
    turned = pltpu.roll(vector, columns // 2, 1)
    turned = jnp.where(lane_is_real(vector.shape), turned, -turned)
    scratch[pl.ds(0, rows, stride=2), :] = vector
    scratch[pl.ds(1, rows, stride=2), :] = turned
    return scratch[...].astype(jnp.bfloat16)


def combine(scratch):
    rows = scratch.shape[0] // 2
    plain = scratch[pl.ds(0, rows, stride=2), :]
    turned = pltpu.roll(scratch[pl.ds(1, rows, stride=2), :], scratch.shape[1] // 2, 1)
    return plain + jnp.where(lane_is_real(plain.shape), -turned, turned)


def contract(basis, vectors, ranks, out):
    inside, slots, _ = out.shape
    product = lax.dot_general(
        basis, vectors, (((0,), (0,)), ((), ())), preferred_element_type=jnp.float32
    )
    level = lax.broadcasted_iota(jnp.int32, (slots, out.shape[2]), 0)
    for tile in range(inside):
        piece = product[tile * slots : (tile + 1) * slots]
        out[tile] = jnp.where(level < ranks[tile], piece, 0.0).astype(out.dtype)


def planes_as_rows(basis):
    height, planes, columns = basis.shape
    return basis.reshape(height * planes, columns)


def partials_kernel(ranks, basis, vector, out, pairs):
    vectors = interleave(vector[0].astype(jnp.float32), pairs)
    contract(planes_as_rows(basis[0]), vectors, ranks, out)


def partials(basis, vector, ranks, freq):
    _, height, planes, columns = basis.shape
    inside = ranks.shape[0]
    width = vector.shape[2]
    return pl.pallas_call(
        partials_kernel,
        grid=(1,),
        in_specs=[
            pl.BlockSpec(memory_space=pltpu.SMEM),
            pl.BlockSpec((1, height, planes, columns), lambda _: (freq, 0, 0, 0)),
            pl.BlockSpec((1, height, width), lambda _: (freq, 0, 0)),
        ],
        out_specs=pl.BlockSpec((inside, columns // inside, width), lambda _: (0, 0, 0)),
        out_shape=jax.ShapeDtypeStruct((inside, columns // inside, width), jnp.bfloat16),
        scratch_shapes=[pltpu.VMEM((height * planes, width), jnp.float32)],
        name="partials",
    )(ranks, basis, vector)


def residual_kernel(ranks, basis, coefficient, recorded, *rest):
    misfit, out, product, pairs = rest[-4:]
    rows = planes_as_rows(basis[0])
    inside, slots, width = coefficient.shape
    product[...] = jnp.dot(
        rows, coefficient[...].reshape(inside * slots, width), preferred_element_type=jnp.float32
    )
    value = combine(product) - recorded[0]
    misfit[0] = value
    contract(rows, interleave(value, pairs), ranks, out)


def residual(basis, coefficient, recorded, ranks, freq, before):
    freqs, height, planes, columns = basis.shape
    inside, slots, width = coefficient.shape
    operands = [ranks, basis, coefficient, recorded]
    in_specs = [
        pl.BlockSpec(memory_space=pltpu.SMEM),
        pl.BlockSpec((1, height, planes, columns), lambda _: (freq, 0, 0, 0)),
        pl.BlockSpec((inside, slots, width), lambda _: (0, 0, 0)),
        pl.BlockSpec((1, height, width), lambda _: (freq, 0, 0)),
    ]
    aliases = {}
    if before is not None:
        aliases = {len(operands): 0}
        operands.append(before)
        in_specs.append(pl.BlockSpec(memory_space=pl.ANY))
    return pl.pallas_call(
        residual_kernel,
        grid=(1,),
        in_specs=in_specs,
        out_specs=[
            pl.BlockSpec((1, height, width), lambda _: (freq, 0, 0)),
            pl.BlockSpec((inside, slots, width), lambda _: (0, 0, 0)),
        ],
        out_shape=[
            jax.ShapeDtypeStruct((freqs, height, width), jnp.float32),
            jax.ShapeDtypeStruct((inside, slots, width), jnp.bfloat16),
        ],
        scratch_shapes=[
            pltpu.VMEM((height * planes, width), jnp.float32),
            pltpu.VMEM((height * planes, width), jnp.float32),
        ],
        input_output_aliases=aliases,
        name="residual",
    )(*operands)


def update_kernel(basis, coefficient, model, out, product):
    inside, slots, width = coefficient.shape
    product[...] = jnp.dot(
        planes_as_rows(basis[0]),
        coefficient[...].reshape(inside * slots, width),
        preferred_element_type=jnp.float32,
    )
    out[...] = (model[0] - STEP_SIZE * combine(product)).astype(out.dtype)


def update(basis, coefficient, model, freq):
    _, height, planes, columns = basis.shape
    inside, slots, width = coefficient.shape
    return pl.pallas_call(
        update_kernel,
        grid=(1,),
        in_specs=[
            pl.BlockSpec((1, height, planes, columns), lambda _: (freq, 0, 0, 0)),
            pl.BlockSpec((inside, slots, width), lambda _: (0, 0, 0)),
            pl.BlockSpec((1, height, width), lambda _: (freq, 0, 0)),
        ],
        out_specs=pl.BlockSpec((height, width), lambda _: (0, 0)),
        out_shape=jax.ShapeDtypeStruct((height, width), jnp.bfloat16),
        scratch_shapes=[pltpu.VMEM((height * planes, width), jnp.float32)],
        name="update",
    )(basis, coefficient, model)


def sparsify_kernel(mute, cutoff, ahead, back, *rest):
    spread, (out, planes, returned) = rest[:-3], rest[-3:]
    freq_count = len(spread)
    rows, width = spread[0].shape
    half = rows // 2
    kept = out.shape[0]
    terms, sums = 2 * freq_count, returned.shape[0] // half
    is_real = lane_is_real((half, width))
    for k in range(freq_count):
        upper = spread[k][:half].astype(jnp.float32)
        lower = spread[k][half:].astype(jnp.float32)
        planes[pl.ds(2 * k, half, stride=terms), :] = jnp.where(
            is_real, upper, pltpu.roll(lower, width // 2, 1)
        )
        planes[pl.ds(2 * k + 1, half, stride=terms), :] = jnp.where(
            is_real, pltpu.roll(upper, width // 2, 1), lower
        )
    limit = jnp.concatenate([cutoff[...], cutoff[...]], 1)
    sample_index = lax.broadcasted_iota(jnp.int32, (NT // 2, 2 * width), 0)
    ahead_early, ahead_late = ahead[: NT // 2], ahead[NT // 2 :]

    def per_pair(step, _):
        first = 2 * step
        pair = planes[pl.ds(pl.multiple_of(first * terms, 2 * terms), 2 * terms), :]
        values = jnp.concatenate([pair[:terms], pair[terms:]], 1).astype(jnp.bfloat16)
        starts = jnp.concatenate([mute[pl.ds(first, 1), :], mute[pl.ds(first + 1, 1), :]], 1)
        early = jnp.dot(ahead_early, values, preferred_element_type=jnp.float32)
        late = jnp.dot(ahead_late, values, preferred_element_type=jnp.float32)
        early = early - jnp.clip(early, -limit, limit)
        early = jnp.where(sample_index >= starts, early, 0.0)
        late = late - jnp.clip(late, -limit, limit)
        series = jnp.concatenate([early, late], 0).astype(jnp.bfloat16)
        sums_here = jnp.dot(back[...], series, preferred_element_type=jnp.float32)
        returned[pl.ds(pl.multiple_of(first * sums, 2 * sums), 2 * sums), :] = jnp.concatenate(
            [sums_here[:, :width], sums_here[:, width:]], 0
        )
        return 0

    lax.fori_loop(0, half // 2, per_pair, 0, unroll=4)
    for k in range(kept):
        real_part = returned[pl.ds(2 * k, half, stride=sums), :]
        imag_part = returned[pl.ds(2 * k + 1, half, stride=sums), :]
        out[k, :half] = jnp.where(is_real, real_part, pltpu.roll(imag_part, width // 2, 1))
        out[k, half:] = jnp.where(is_real, pltpu.roll(real_part, width // 2, 1), imag_part)


def sparsify(spread, mute, cutoff, ahead, back, kept):
    rows, width = spread[0].shape
    terms, sums = 2 * len(spread), back.shape[0]
    return pl.pallas_call(
        sparsify_kernel,
        out_shape=jax.ShapeDtypeStruct((kept, rows, width), jnp.float32),
        scratch_shapes=[
            pltpu.VMEM((rows // 2 * terms, width), jnp.float32),
            pltpu.VMEM((rows // 2 * sums, width), jnp.float32),
        ],
        name="sparsify",
    )(mute, cutoff, ahead, back, *spread)


def wave_tables(freq_count, kept):
    sample_index = lax.iota(jnp.int32, NT)[:, None]
    order = (lax.iota(jnp.int32, freq_count) + kept * lax.axis_index("freq")) % freq_count
    phases = (sample_index * (order[None, :] + NT // 4) % NT).astype(jnp.float32)
    phases = phases * (2.0 * math.pi / NT)
    table = jnp.stack([jnp.cos(phases), -jnp.sin(phases)], 2).reshape(NT, 2 * freq_count)
    ahead = (table / math.sqrt(freq_count)).astype(jnp.bfloat16)
    sums = -(-2 * kept // 8) * 8
    back = (table[:, : 2 * kept] * (2.0 * math.sqrt(freq_count) / NT)).T
    back = jnp.pad(back, ((0, sums - 2 * kept), (0, 0))).astype(jnp.bfloat16)
    return ahead, back


def shuffle(partial_value):
    inside, slots, columns = partial_value.shape
    tile_count = lax.axis_size("tile")
    group_size = tile_count // inside
    if group_size == 1:
        return lax.all_to_all(partial_value, "tile", split_axis=0, concat_axis=0, tiled=True)
    outgoing = jnp.broadcast_to(partial_value[:, None], (inside, group_size, slots, columns))
    outgoing = outgoing.reshape(tile_count, slots, columns)
    incoming = lax.all_to_all(outgoing, "tile", split_axis=0, concat_axis=0, tiled=True)
    incoming = incoming.reshape(inside, group_size, slots, columns).astype(jnp.float32)
    return jnp.sum(incoming, 1).astype(jnp.bfloat16)


def from_others(value):
    size = lax.axis_size("freq")
    return [
        lax.ppermute(value, "freq", [((d + shift) % size, d) for d in range(size)])
        for shift in range(1, size)
    ]


def body(left_basis, right_basis, start_model, recorded, tile_ranks, mute_start, thresholds):
    tile_count = lax.axis_size("tile")
    inside = tile_ranks.shape[0]
    tile_block = lax.axis_index("tile") // (tile_count // inside)
    column_ranks = lax.dynamic_slice_in_dim(tile_ranks, tile_block, 1, 1).reshape(inside)
    row_ranks = lax.dynamic_slice_in_dim(tile_ranks, tile_block, 1, 0).reshape(inside)
    kept, height, width = start_model.shape
    freq_count = kept * lax.axis_size("freq")
    half = height // 2
    mute = jnp.concatenate([mute_start[:half], mute_start[half:]], 1)
    cutoff = jnp.tile(thresholds, 2)[None]
    ahead, back = wave_tables(freq_count, kept)
    freqs = range(kept)
    model = start_model
    for outer_step in range(OUTER):
        forward = [shuffle(partials(right_basis, model, column_ranks, f)) for f in freqs]
        misfit = None
        adjoint = []
        for f in freqs:
            misfit, outgoing = residual(left_basis, forward[f], recorded, row_ranks, f, misfit)
            adjoint.append(shuffle(outgoing))
        own, others = [], []
        for f in freqs:
            own.append(update(right_basis, adjoint[f], model, f))
            others.append(from_others(own[f]))
        spread = own + [others[f][d] for d in range(len(others[0])) for f in freqs]
        model = sparsify(spread, mute, cutoff, ahead, back, kept)
    return (model, misfit)


def solution(mesh):
    return jax.shard_map(
        body,
        mesh=mesh,
        in_specs=(
            P("freq", "tile", None, None),
            P("freq", "tile", None, None),
            P("freq", "tile", None),
            P("freq", "tile", None),
            P(),
            P("tile", None),
            P(),
        ),
        out_specs=(P("freq", "tile", None), P("freq", "tile", None)),
        check_vma=False,
    )
```

profile of v0, /device:TPU:0, one launch (start us, length us, event | category | flops | bytes accessed | tf_op | source)
XLA Modules:
  0.0 216.2 jit_solution(1008290331151598070)
XLA Ops:
  2.1 3.8 %partials.4 = bf16[16,96,128]{2,1,0:T(8,128)(2,1)} custom-call(s32[16]{0:T(128)} %dynamic-slice_reduce_fusion.ranks, bf16[2,512,2,1536]{3,2,1,0:T(2,128)(2,1)} %basis.23, f32[2,512,128]{2,1,0:T(8,128)} %model.3), custom_call_target="tpu_custom_call" | custom-call | tf_op jit(solution)/shard_map/partials/pallas_call | solution.py:60
  5.9 7.4 %all-to-all-start = ((bf16[16,96,128]{2,1,0:T(8,128)(2,1)}), bf16[16,96,128]{2,1,0:T(8,128)(2,1)S(1)}, u32[]{:S(2)}, u32[]{:S(2)}) async-start(bf16[16,96,128]{2,1,0:T(8,128)(2,1)} %partials.4), calls=%async_computation | async-start | bytes 786432 | tf_op jit(solution)/shard_map/all_to_all | solution.py:229
  13.4 3.9 %partials.5 = bf16[16,96,128]{2,1,0:T(8,128)(2,1)} custom-call(s32[16]{0:T(128)} %dynamic-slice_reduce_fusion.ranks, bf16[2,512,2,1536]{3,2,1,0:T(2,128)(2,1)} %basis.23, f32[2,512,128]{2,1,0:T(8,128)} %model.3), custom_call_target="tpu_custom_call" | custom-call | tf_op jit(solution)/shard_map/partials/pallas_call | solution.py:60
  17.2 8.3 %all-to-all-done.coefficient = bf16[16,96,128]{2,1,0:T(8,128)(2,1)S(1)} async-done(((bf16[16,96,128]{2,1,0:T(8,128)(2,1)}), bf16[16,96,128]{2,1,0:T(8,128)(2,1)S(1)}, u32[]{:S(2)}, u32[]{:S(2)}) %all-to-all-start) | async-done | bytes 393248 | tf_op jit(solution)/shard_map/all_to_all | solution.py:229
  25.5 3.6 %all-to-all-start.2 = ((bf16[16,96,128]{2,1,0:T(8,128)(2,1)}), bf16[16,96,128]{2,1,0:T(8,128)(2,1)S(1)}, u32[]{:S(2)}, u32[]{:S(2)}) async-start(bf16[16,96,128]{2,1,0:T(8,128)(2,1)} %partials.5), calls=%async_computation.2 | async-start | bytes 786432 | tf_op jit(solution)/shard_map/all_to_all | solution.py:229
  29.6 6.3 %residual.4 = (f32[2,512,128]{2,1,0:T(8,128)}, bf16[16,96,128]{2,1,0:T(8,128)(2,1)}) custom-call(s32[16]{0:T(128)} %dynamic-slice_bitcast_fusion.ranks, bf16[2,512,2,1536]{3,2,1,0:T(2,128)(2,1)} %basis.22, bf16[16,96,128]{2,1,0:T(8,128)(2,1)} %copy-done.6, f32[2,512,128]{2,1,0:T(8,128)} %recorded.7), custom_call_target="tpu_custom_call" | custom-call | tf_op jit(solution)/shard_map/residual/pallas_call | solution.py:102
  35.9 5.3 %all-to-all-done.2.coefficient = bf16[16,96,128]{2,1,0:T(8,128)(2,1)S(1)} async-done(((bf16[16,96,128]{2,1,0:T(8,128)(2,1)}), bf16[16,96,128]{2,1,0:T(8,128)(2,1)S(1)}, u32[]{:S(2)}, u32[]{:S(2)}) %all-to-all-start.2) | async-done | bytes 393248 | tf_op jit(solution)/shard_map/all_to_all | solution.py:229
  41.2 3.6 %all-to-all-start.1 = ((bf16[16,96,128]{2,1,0:T(8,128)(2,1)}), bf16[16,96,128]{2,1,0:T(8,128)(2,1)S(1)}, u32[]{:S(2)}, u32[]{:S(2)}) async-start(bf16[16,96,128]{2,1,0:T(8,128)(2,1)} %get-tuple-element.9), calls=%async_computation.1 | async-start | bytes 786432 | tf_op jit(solution)/shard_map/all_to_all | solution.py:229
  44.8 6.3 %residual.5 = (f32[2,512,128]{2,1,0:T(8,128)}, bf16[16,96,128]{2,1,0:T(8,128)(2,1)}) custom-call(s32[16]{0:T(128)} %dynamic-slice_bitcast_fusion.ranks, bf16[2,512,2,1536]{3,2,1,0:T(2,128)(2,1)} %basis.22, bf16[16,96,128]{2,1,0:T(8,128)(2,1)} %copy-done.2, f32[2,512,128]{2,1,0:T(8,128)} %recorded.7, ...), custom_call_target="tpu_custom_call", output_to_operand_aliasing={{0}: (4, {})} | custom-call | tf_op jit(solution)/shard_map/residual/pallas_call | solution.py:102
  51.1 5.8 %all-to-all-done.1.coefficient = bf16[16,96,128]{2,1,0:T(8,128)(2,1)S(1)} async-done(((bf16[16,96,128]{2,1,0:T(8,128)(2,1)}), bf16[16,96,128]{2,1,0:T(8,128)(2,1)S(1)}, u32[]{:S(2)}, u32[]{:S(2)}) %all-to-all-start.1) | async-done | bytes 393248 | tf_op jit(solution)/shard_map/all_to_all | solution.py:229
  56.9 3.7 %all-to-all-start.3 = ((bf16[16,96,128]{2,1,0:T(8,128)(2,1)}), bf16[16,96,128]{2,1,0:T(8,128)(2,1)S(1)}, u32[]{:S(2)}, u32[]{:S(2)}) async-start(bf16[16,96,128]{2,1,0:T(8,128)(2,1)} %get-tuple-element.11), calls=%async_computation.3 | async-start | bytes 786432 | tf_op jit(solution)/shard_map/all_to_all | solution.py:229
  60.9 3.9 %update.4.rest_0_ = bf16[512,128]{1,0:T(8,128)(2,1)} custom-call(bf16[2,512,2,1536]{3,2,1,0:T(2,128)(2,1)} %basis.23, bf16[16,96,128]{2,1,0:T(8,128)(2,1)} %copy-done.1, f32[2,512,128]{2,1,0:T(8,128)} %model.3), custom_call_target="tpu_custom_call" | custom-call | tf_op jit(solution)/shard_map/update/pallas_call | solution.py:136
  66.2 6.4 %all-to-all-done.3.coefficient = bf16[16,96,128]{2,1,0:T(8,128)(2,1)S(1)} async-done(((bf16[16,96,128]{2,1,0:T(8,128)(2,1)}), bf16[16,96,128]{2,1,0:T(8,128)(2,1)S(1)}, u32[]{:S(2)}, u32[]{:S(2)}) %all-to-all-start.3) | async-done | bytes 393248 | tf_op jit(solution)/shard_map/all_to_all | solution.py:229
  73.3 3.8 %update.5.rest_1_ = bf16[512,128]{1,0:T(8,128)(2,1)} custom-call(bf16[2,512,2,1536]{3,2,1,0:T(2,128)(2,1)} %basis.23, bf16[16,96,128]{2,1,0:T(8,128)(2,1)} %copy-done.3, f32[2,512,128]{2,1,0:T(8,128)} %model.3), custom_call_target="tpu_custom_call" | custom-call | tf_op jit(solution)/shard_map/update/pallas_call | solution.py:136
  83.6 27.4 %sparsify.2.vector.model = f32[2,512,128]{2,1,0:T(8,128)} custom-call(s32[256,128]{1,0:T(8,128)} %pad_add_fusion.mute, f32[1,128]{1,0:T(1,128)} %broadcast_in_dim_tile.3.cutoff, bf16[256,8]{1,0:T(8,128)(2,1)} %copy.23.ahead, bf16[8,256]{1,0:T(8,128)(2,1)} %pad.5.back, bf16[512,128]{1,0:T(8,128)(2,1)} %update.4.rest_0_, bf16[512,128]{1,0:T(8,128)(2,1)} %update.5.rest_1_, ...), custom_call_target="tpu_custom_call" | custom-call | tf_op jit(solution)/shard_map/sparsify/pallas_call | solution.py:200
  111.0 3.8 %partials.6 = bf16[16,96,128]{2,1,0:T(8,128)(2,1)} custom-call(s32[16]{0:T(128)} %dynamic-slice_reduce_fusion.ranks, bf16[2,512,2,1536]{3,2,1,0:T(2,128)(2,1)} %basis.23, f32[2,512,128]{2,1,0:T(8,128)} %sparsify.2.vector.model), custom_call_target="tpu_custom_call" | custom-call | tf_op jit(solution)/shard_map/partials/pallas_call | solution.py:60
  114.9 3.6 %all-to-all-start.4 = ((bf16[16,96,128]{2,1,0:T(8,128)(2,1)}), bf16[16,96,128]{2,1,0:T(8,128)(2,1)S(1)}, u32[]{:S(2)}, u32[]{:S(2)}) async-start(bf16[16,96,128]{2,1,0:T(8,128)(2,1)} %partials.6), calls=%async_computation.4 | async-start | bytes 786432 | tf_op jit(solution)/shard_map/all_to_all | solution.py:229
  118.5 3.9 %partials.7 = bf16[16,96,128]{2,1,0:T(8,128)(2,1)} custom-call(s32[16]{0:T(128)} %dynamic-slice_reduce_fusion.ranks, bf16[2,512,2,1536]{3,2,1,0:T(2,128)(2,1)} %basis.23, f32[2,512,128]{2,1,0:T(8,128)} %sparsify.2.vector.model), custom_call_target="tpu_custom_call" | custom-call | tf_op jit(solution)/shard_map/partials/pallas_call | solution.py:60
  122.4 8.3 %all-to-all-done.4.coefficient = bf16[16,96,128]{2,1,0:T(8,128)(2,1)S(1)} async-done(((bf16[16,96,128]{2,1,0:T(8,128)(2,1)}), bf16[16,96,128]{2,1,0:T(8,128)(2,1)S(1)}, u32[]{:S(2)}, u32[]{:S(2)}) %all-to-all-start.4) | async-done | bytes 393248 | tf_op jit(solution)/shard_map/all_to_all | solution.py:229
  130.7 3.6 %all-to-all-start.6 = ((bf16[16,96,128]{2,1,0:T(8,128)(2,1)}), bf16[16,96,128]{2,1,0:T(8,128)(2,1)S(1)}, u32[]{:S(2)}, u32[]{:S(2)}) async-start(bf16[16,96,128]{2,1,0:T(8,128)(2,1)} %partials.7), calls=%async_computation.6 | async-start | bytes 786432 | tf_op jit(solution)/shard_map/all_to_all | solution.py:229
  134.3 6.3 %residual.6 = (f32[2,512,128]{2,1,0:T(8,128)}, bf16[16,96,128]{2,1,0:T(8,128)(2,1)}) custom-call(s32[16]{0:T(128)} %dynamic-slice_bitcast_fusion.ranks, bf16[2,512,2,1536]{3,2,1,0:T(2,128)(2,1)} %basis.22, bf16[16,96,128]{2,1,0:T(8,128)(2,1)} %copy-done.7, f32[2,512,128]{2,1,0:T(8,128)} %recorded.7), custom_call_target="tpu_custom_call" | custom-call | tf_op jit(solution)/shard_map/residual/pallas_call | solution.py:102
  140.6 5.8 %all-to-all-done.6.coefficient = bf16[16,96,128]{2,1,0:T(8,128)(2,1)S(1)} async-done(((bf16[16,96,128]{2,1,0:T(8,128)(2,1)}), bf16[16,96,128]{2,1,0:T(8,128)(2,1)S(1)}, u32[]{:S(2)}, u32[]{:S(2)}) %all-to-all-start.6) | async-done | bytes 393248 | tf_op jit(solution)/shard_map/all_to_all | solution.py:229
  146.4 3.8 %all-to-all-start.5 = ((bf16[16,96,128]{2,1,0:T(8,128)(2,1)}), bf16[16,96,128]{2,1,0:T(8,128)(2,1)S(1)}, u32[]{:S(2)}, u32[]{:S(2)}) async-start(bf16[16,96,128]{2,1,0:T(8,128)(2,1)} %get-tuple-element.12), calls=%async_computation.5 | async-start | bytes 786432 | tf_op jit(solution)/shard_map/all_to_all | solution.py:229
  150.2 6.3 %residual.7 = (f32[2,512,128]{2,1,0:T(8,128)}, bf16[16,96,128]{2,1,0:T(8,128)(2,1)}) custom-call(s32[16]{0:T(128)} %dynamic-slice_bitcast_fusion.ranks, bf16[2,512,2,1536]{3,2,1,0:T(2,128)(2,1)} %basis.22, bf16[16,96,128]{2,1,0:T(8,128)(2,1)} %copy-done.4, f32[2,512,128]{2,1,0:T(8,128)} %recorded.7, ...), custom_call_target="tpu_custom_call", output_to_operand_aliasing={{0}: (4, {})} | custom-call | tf_op jit(solution)/shard_map/residual/pallas_call | solution.py:102
  156.5 5.6 %all-to-all-done.5.coefficient = bf16[16,96,128]{2,1,0:T(8,128)(2,1)S(1)} async-done(((bf16[16,96,128]{2,1,0:T(8,128)(2,1)}), bf16[16,96,128]{2,1,0:T(8,128)(2,1)S(1)}, u32[]{:S(2)}, u32[]{:S(2)}) %all-to-all-start.5) | async-done | bytes 393248 | tf_op jit(solution)/shard_map/all_to_all | solution.py:229
  162.1 3.6 %all-to-all-start.7 = ((bf16[16,96,128]{2,1,0:T(8,128)(2,1)}), bf16[16,96,128]{2,1,0:T(8,128)(2,1)S(1)}, u32[]{:S(2)}, u32[]{:S(2)}) async-start(bf16[16,96,128]{2,1,0:T(8,128)(2,1)} %get-tuple-element.14), calls=%async_computation.7 | async-start | bytes 786432 | tf_op jit(solution)/shard_map/all_to_all | solution.py:229
  165.6 3.9 %update.6.rest_0_ = bf16[512,128]{1,0:T(8,128)(2,1)} custom-call(bf16[2,512,2,1536]{3,2,1,0:T(2,128)(2,1)} %basis.23, bf16[16,96,128]{2,1,0:T(8,128)(2,1)} %copy-done.5, f32[2,512,128]{2,1,0:T(8,128)} %sparsify.2.vector.model), custom_call_target="tpu_custom_call" | custom-call | tf_op jit(solution)/shard_map/update/pallas_call | solution.py:136
  169.5 1.5 collective-permute-start.2
  171.0 6.8 %all-to-all-done.7.coefficient = bf16[16,96,128]{2,1,0:T(8,128)(2,1)S(1)} async-done(((bf16[16,96,128]{2,1,0:T(8,128)(2,1)}), bf16[16,96,128]{2,1,0:T(8,128)(2,1)S(1)}, u32[]{:S(2)}, u32[]{:S(2)}) %all-to-all-start.7) | async-done | bytes 393248 | tf_op jit(solution)/shard_map/all_to_all | solution.py:229
  178.5 3.8 %update.7.rest_1_ = bf16[512,128]{1,0:T(8,128)(2,1)} custom-call(bf16[2,512,2,1536]{3,2,1,0:T(2,128)(2,1)} %basis.23, bf16[16,96,128]{2,1,0:T(8,128)(2,1)} %copy-done.8, f32[2,512,128]{2,1,0:T(8,128)} %sparsify.2.vector.model), custom_call_target="tpu_custom_call" | custom-call | tf_op jit(solution)/shard_map/update/pallas_call | solution.py:136
  183.9 4.2 %collective-permute-done.3.rest_3_ = bf16[512,128]{1,0:T(8,128)(2,1)S(1)} collective-permute-done((bf16[512,128]{1,0:T(8,128)(2,1)}, bf16[512,128]{1,0:T(8,128)(2,1)S(1)}, u32[]{:S(2)}, u32[]{:S(2)}) %collective-permute-start.3) | collective-permute-done | bytes 131104 | tf_op jit(solution)/shard_map/ppermute | solution.py:240
  188.7 27.4 %sparsify.3 = f32[2,512,128]{2,1,0:T(8,128)} custom-call(s32[256,128]{1,0:T(8,128)} %pad_add_fusion.mute, f32[1,128]{1,0:T(1,128)} %broadcast_in_dim_tile.3.cutoff, bf16[256,8]{1,0:T(8,128)(2,1)} %copy.23.ahead, bf16[8,256]{1,0:T(8,128)(2,1)} %pad.5.back, bf16[512,128]{1,0:T(8,128)(2,1)} %update.6.rest_0_, bf16[512,128]{1,0:T(8,128)(2,1)} %update.7.rest_1_, ...), custom_call_target="tpu_custom_call" | custom-call | tf_op jit(solution)/shard_map/sparsify/pallas_call | solution.py:200
  (53 shorter events, 13.6 us)
Async XLA Ops:
  0.6 0.7 copy-start
  5.9 19.6 %all-to-all-start = ((bf16[16,96,128]{2,1,0:T(8,128)(2,1)}), bf16[16,96,128]{2,1,0:T(8,128)(2,1)S(1)}, u32[]{:S(2)}, u32[]{:S(2)}) async-start(bf16[16,96,128]{2,1,0:T(8,128)(2,1)} %partials.4), calls=%async_computation | async-start | bytes 786432 | tf_op jit(solution)/shard_map/all_to_all | solution.py:229
  25.5 4.1 %copy-start.6 = (bf16[16,96,128]{2,1,0:T(8,128)(2,1)}, bf16[16,96,128]{2,1,0:T(8,128)(2,1)S(1)}, u32[]{:S(2)}) copy-start(bf16[16,96,128]{2,1,0:T(8,128)(2,1)S(1)} %all-to-all-done.coefficient) | copy-start | bytes 1179652
  25.5 15.7 %all-to-all-start.2 = ((bf16[16,96,128]{2,1,0:T(8,128)(2,1)}), bf16[16,96,128]{2,1,0:T(8,128)(2,1)S(1)}, u32[]{:S(2)}, u32[]{:S(2)}) async-start(bf16[16,96,128]{2,1,0:T(8,128)(2,1)} %partials.5), calls=%async_computation.2 | async-start | bytes 786432 | tf_op jit(solution)/shard_map/all_to_all | solution.py:229
  35.9 24.9 %copy-start.13 = (s32[512,64]{0,1:T(8,128)S(1)}, s32[512,64]{0,1:T(8,128)}, u32[]{:S(2)}) copy-start(s32[512,64]{0,1:T(8,128)} %param.12) | copy-start | bytes 393220
  41.2 3.6 %copy-start.2 = (bf16[16,96,128]{2,1,0:T(8,128)(2,1)}, bf16[16,96,128]{2,1,0:T(8,128)(2,1)S(1)}, u32[]{:S(2)}) copy-start(bf16[16,96,128]{2,1,0:T(8,128)(2,1)S(1)} %all-to-all-done.2.coefficient) | copy-start | bytes 1179652
  41.2 15.7 %all-to-all-start.1 = ((bf16[16,96,128]{2,1,0:T(8,128)(2,1)}), bf16[16,96,128]{2,1,0:T(8,128)(2,1)S(1)}, u32[]{:S(2)}, u32[]{:S(2)}) async-start(bf16[16,96,128]{2,1,0:T(8,128)(2,1)} %get-tuple-element.9), calls=%async_computation.1 | async-start | bytes 786432 | tf_op jit(solution)/shard_map/all_to_all | solution.py:229
  56.9 4.0 %copy-start.1 = (bf16[16,96,128]{2,1,0:T(8,128)(2,1)}, bf16[16,96,128]{2,1,0:T(8,128)(2,1)S(1)}, u32[]{:S(2)}) copy-start(bf16[16,96,128]{2,1,0:T(8,128)(2,1)S(1)} %all-to-all-done.1.coefficient) | copy-start | bytes 1179652
  56.9 15.7 %all-to-all-start.3 = ((bf16[16,96,128]{2,1,0:T(8,128)(2,1)}), bf16[16,96,128]{2,1,0:T(8,128)(2,1)S(1)}, u32[]{:S(2)}, u32[]{:S(2)}) async-start(bf16[16,96,128]{2,1,0:T(8,128)(2,1)} %get-tuple-element.11), calls=%async_computation.3 | async-start | bytes 786432 | tf_op jit(solution)/shard_map/all_to_all | solution.py:229
  60.9 18.0 %copy-start.14 = (f32[64]{0:T(128)S(1)}, f32[64]{0:T(128)}, u32[]{:S(2)}) copy-start(f32[64]{0:T(128)} %param.13) | copy-start | bytes 772
  64.7 16.9 %collective-permute-start = (bf16[512,128]{1,0:T(8,128)(2,1)}, bf16[512,128]{1,0:T(8,128)(2,1)S(1)}, u32[]{:S(2)}, u32[]{:S(2)}) collective-permute-start(bf16[512,128]{1,0:T(8,128)(2,1)} %update.4.rest_0_), channel_id=1, source_target_pairs={{16,0},{0,16},{17,1},{1,17},{18,2},{2,18},{19,3},{3,19},{20,4},{4,... | collective-permute-start | bytes 393224 | tf_op jit(solution)/shard_map/ppermute | solution.py:240
  72.6 0.7 copy-start.3
  77.2 5.7 %collective-permute-start.1 = (bf16[512,128]{1,0:T(8,128)(2,1)}, bf16[512,128]{1,0:T(8,128)(2,1)S(1)}, u32[]{:S(2)}, u32[]{:S(2)}) collective-permute-start(bf16[512,128]{1,0:T(8,128)(2,1)} %update.5.rest_1_), channel_id=1, source_target_pairs={{16,0},{0,16},{17,1},{1,17},{18,2},{2,18},{19,3},{3,19},{20,4},{4,... | collective-permute-start | bytes 393224 | tf_op jit(solution)/shard_map/ppermute | solution.py:240
  81.6 1.3 copy-start.9
  82.9 0.7 copy-start.10
  114.9 15.8 %all-to-all-start.4 = ((bf16[16,96,128]{2,1,0:T(8,128)(2,1)}), bf16[16,96,128]{2,1,0:T(8,128)(2,1)S(1)}, u32[]{:S(2)}, u32[]{:S(2)}) async-start(bf16[16,96,128]{2,1,0:T(8,128)(2,1)} %partials.6), calls=%async_computation.4 | async-start | bytes 786432 | tf_op jit(solution)/shard_map/all_to_all | solution.py:229
  130.7 3.6 %copy-start.7 = (bf16[16,96,128]{2,1,0:T(8,128)(2,1)}, bf16[16,96,128]{2,1,0:T(8,128)(2,1)S(1)}, u32[]{:S(2)}) copy-start(bf16[16,96,128]{2,1,0:T(8,128)(2,1)S(1)} %all-to-all-done.4.coefficient) | copy-start | bytes 1179652
  130.7 15.7 %all-to-all-start.6 = ((bf16[16,96,128]{2,1,0:T(8,128)(2,1)}), bf16[16,96,128]{2,1,0:T(8,128)(2,1)S(1)}, u32[]{:S(2)}, u32[]{:S(2)}) async-start(bf16[16,96,128]{2,1,0:T(8,128)(2,1)} %partials.7), calls=%async_computation.6 | async-start | bytes 786432 | tf_op jit(solution)/shard_map/all_to_all | solution.py:229
  146.4 3.8 %copy-start.4 = (bf16[16,96,128]{2,1,0:T(8,128)(2,1)}, bf16[16,96,128]{2,1,0:T(8,128)(2,1)S(1)}, u32[]{:S(2)}) copy-start(bf16[16,96,128]{2,1,0:T(8,128)(2,1)S(1)} %all-to-all-done.6.coefficient) | copy-start | bytes 1179652
  146.4 15.7 %all-to-all-start.5 = ((bf16[16,96,128]{2,1,0:T(8,128)(2,1)}), bf16[16,96,128]{2,1,0:T(8,128)(2,1)S(1)}, u32[]{:S(2)}, u32[]{:S(2)}) async-start(bf16[16,96,128]{2,1,0:T(8,128)(2,1)} %get-tuple-element.12), calls=%async_computation.5 | async-start | bytes 786432 | tf_op jit(solution)/shard_map/all_to_all | solution.py:229
  162.1 3.6 %copy-start.5 = (bf16[16,96,128]{2,1,0:T(8,128)(2,1)}, bf16[16,96,128]{2,1,0:T(8,128)(2,1)S(1)}, u32[]{:S(2)}) copy-start(bf16[16,96,128]{2,1,0:T(8,128)(2,1)S(1)} %all-to-all-done.5.coefficient) | copy-start | bytes 1179652
  162.1 15.7 %all-to-all-start.7 = ((bf16[16,96,128]{2,1,0:T(8,128)(2,1)}), bf16[16,96,128]{2,1,0:T(8,128)(2,1)S(1)}, u32[]{:S(2)}, u32[]{:S(2)}) async-start(bf16[16,96,128]{2,1,0:T(8,128)(2,1)} %get-tuple-element.14), calls=%async_computation.7 | async-start | bytes 786432 | tf_op jit(solution)/shard_map/all_to_all | solution.py:229
  169.5 14.4 %collective-permute-start.2 = (bf16[512,128]{1,0:T(8,128)(2,1)}, bf16[512,128]{1,0:T(8,128)(2,1)S(1)}, u32[]{:S(2)}, u32[]{:S(2)}) collective-permute-start(bf16[512,128]{1,0:T(8,128)(2,1)} %update.6.rest_0_), channel_id=1, source_target_pairs={{16,0},{0,16},{17,1},{1,17},{18,2},{2,18},{19,3},{3,19},{20,4},{4,... | collective-permute-start | bytes 393224 | tf_op jit(solution)/shard_map/ppermute | solution.py:240
  177.8 0.8 copy-start.8
  182.4 5.7 %collective-permute-start.3 = (bf16[512,128]{1,0:T(8,128)(2,1)}, bf16[512,128]{1,0:T(8,128)(2,1)S(1)}, u32[]{:S(2)}, u32[]{:S(2)}) collective-permute-start(bf16[512,128]{1,0:T(8,128)(2,1)} %update.7.rest_1_), channel_id=1, source_target_pairs={{16,0},{0,16},{17,1},{1,17},{18,2},{2,18},{19,3},{3,19},{20,4},{4,... | collective-permute-start | bytes 393224 | tf_op jit(solution)/shard_map/ppermute | solution.py:240
  183.9 4.2 %copy-start.11 = (bf16[512,128]{1,0:T(8,128)(2,1)}, bf16[512,128]{1,0:T(8,128)(2,1)S(1)}, u32[]{:S(2)}) copy-start(bf16[512,128]{1,0:T(8,128)(2,1)S(1)} %collective-permute-done.2.rest_2_) | copy-start | bytes 393220
  188.1 0.6 copy-start.12
where the time goes:
time: 217 us; the launch traced here: 216 us
  Pallas kernels  111 us (51%)
  waiting for transfers between devices  57.7 us (27%)
  starting transfers between devices  38.7 us (18%)
  local copies, waits for them, and re-layouts  6.98 us (3%)
    pallas_call x2, Pallas kernels, sparsify(): pl.pallas_call(sparsify_kernel, out_shape=jax.ShapeDtypeStruct((kept, row...  54.9 us
    all_to_all x8, waiting for transfers between devices, shuffle(): lax.all_to_all(partial_value, 'tile', split_axis=0, concat_axis=0, tiled=...  52.2 us
    all_to_all x8, starting transfers between devices, shuffle(): lax.all_to_all(partial_value, 'tile', split_axis=0, concat_axis=0, tiled=...  32.8 us
    pallas_call x4, Pallas kernels, residual(): pl.pallas_call(residual_kernel, grid=(1,), in_specs=in_specs, out_specs=[...  25.3 us
    pallas_call x4, Pallas kernels, update(): pl.pallas_call(update_kernel, grid=(1,), in_specs=[pl.BlockSpec((1, heigh...  15.4 us
    pallas_call x4, Pallas kernels, partials(): pl.pallas_call(partials_kernel, grid=(1,), in_specs=[pl.BlockSpec(memory_...  15.4 us
    ppermute x4, starting transfers between devices, from_others(): lax.ppermute(value, 'freq', [((d + shift) % size, d) for d in range(size)])  5.97 us
    ppermute x4, waiting for transfers between devices, from_others(): lax.ppermute(value, 'freq', [((d + shift) % size, d) for d in range(size)])  5.51 us
  transfers between devices with their start and end apart: 12, of which 10 were waited for; matrix products, arithmetic and copies ran while one was open for 2% of the time, Pallas kernels for 22%

commit v1 on v0

v1 whole, which is shorter than its diff:
```python
import functools
import math

import jax
import jax.numpy as jnp
from jax import lax
from jax.experimental import pallas as pl
from jax.experimental.pallas import tpu as pltpu
from jax.sharding import PartitionSpec as P

NT = 256
OUTER = 2
STEP_SIZE = 0.5


def lane_is_real(shape):
    return lax.broadcasted_iota(jnp.int32, shape, 1) < shape[1] // 2


def interleave(vector, scratch):
    rows, columns = vector.shape
    turned = pltpu.roll(vector, columns // 2, 1)
    turned = jnp.where(lane_is_real(vector.shape), turned, -turned)
    scratch[pl.ds(0, rows, stride=2), :] = vector
    scratch[pl.ds(1, rows, stride=2), :] = turned
    return scratch[...].astype(jnp.bfloat16)


def combine(scratch):
    rows = scratch.shape[0] // 2
    plain = scratch[pl.ds(0, rows, stride=2), :]
    turned = pltpu.roll(scratch[pl.ds(1, rows, stride=2), :], scratch.shape[1] // 2, 1)
    return plain + jnp.where(lane_is_real(plain.shape), -turned, turned)


def planes_as_rows(basis):
    height, planes, columns = basis.shape
    return basis.reshape(height * planes, columns)


def whole():
    return pl.BlockSpec(memory_space=pltpu.VMEM)


def room(mebibytes):
    return pltpu.CompilerParams(vmem_limit_bytes=mebibytes * 2**20)


def block_of(inside):
    return lax.axis_index("tile") // (lax.axis_size("tile") // inside)


def expand(basis, coefficient, scratch):
    tiles, slots, width = coefficient.shape
    scratch[...] = jnp.dot(
        planes_as_rows(basis),
        coefficient.reshape(tiles * slots, width),
        preferred_element_type=jnp.float32,
    )
    return combine(scratch)


def contract(basis, vector, scratch, rank_of, out):
    tiles, slots, width = out.shape
    vectors = interleave(vector, scratch).T
    product = jnp.dot(vectors, planes_as_rows(basis), preferred_element_type=jnp.float32).T
    level = lax.broadcasted_iota(jnp.int32, (slots, width), 0)
    for tile in range(tiles):
        piece = product[tile * slots : (tile + 1) * slots]
        out[tile] = jnp.where(level < rank_of(tile), piece, 0.0).astype(out.dtype)


def partials_kernel(ranks, basis, vector, out, pairs):
    block = block_of(ranks.shape[0])
    for f in range(basis.shape[0]):
        contract(basis[f], vector[f], pairs, lambda tile: ranks[tile, block], out.at[:, f])


def partials(basis, vector, ranks):
    freqs, height, planes, columns = basis.shape
    inside, width = ranks.shape[0], vector.shape[2]
    return pl.pallas_call(
        partials_kernel,
        in_specs=[pl.BlockSpec(memory_space=pltpu.SMEM), whole(), whole()],
        out_specs=whole(),
        out_shape=jax.ShapeDtypeStruct((inside, freqs, columns // inside, width), jnp.bfloat16),
        scratch_shapes=[pltpu.VMEM((height * planes, width), jnp.float32)],
        compiler_params=room(12),
        name="partials",
    )(ranks, basis, vector)


def residual_kernel(ranks, basis, coefficient, recorded, misfit, out, product, pairs):
    block = block_of(ranks.shape[0])
    for f in range(basis.shape[0]):
        value = expand(basis[f], coefficient[:, f], product) - recorded[f]
        misfit[f] = value
        contract(basis[f], value, pairs, lambda tile: ranks[block, tile], out.at[:, f])


def residual(basis, coefficient, recorded, ranks):
    _, height, planes, _ = basis.shape
    scratch = pltpu.VMEM((height * planes, recorded.shape[2]), jnp.float32)
    return pl.pallas_call(
        residual_kernel,
        in_specs=[pl.BlockSpec(memory_space=pltpu.SMEM), whole(), whole(), whole()],
        out_specs=[whole(), whole()],
        out_shape=[
            jax.ShapeDtypeStruct(recorded.shape, jnp.float32),
            jax.ShapeDtypeStruct(coefficient.shape, jnp.bfloat16),
        ],
        scratch_shapes=[scratch, scratch],
        compiler_params=room(12),
        name="residual",
    )(ranks, basis, coefficient, recorded)


def update_kernel(freq, basis, coefficient, model, out, product):
    gradient = expand(basis[freq], coefficient[:, freq], product)
    out[...] = (model[freq] - STEP_SIZE * gradient).astype(out.dtype)


def update(basis, coefficient, model, freq):
    _, height, planes, _ = basis.shape
    width = model.shape[2]
    return pl.pallas_call(
        functools.partial(update_kernel, freq),
        in_specs=[whole(), whole(), whole()],
        out_specs=whole(),
        out_shape=jax.ShapeDtypeStruct((height, width), jnp.bfloat16),
        scratch_shapes=[pltpu.VMEM((height * planes, width), jnp.float32)],
        compiler_params=room(12),
        name="update",
    )(basis, coefficient, model)


def sparsify_kernel(mute, cutoff, ahead, back, *rest):
    spread, (out, planes, returned, wide, narrow) = rest[:-5], rest[-5:]
    freq_count = len(spread)
    rows, width = spread[0].shape
    half = rows // 2
    kept = out.shape[0]
    terms, sums = 2 * freq_count, returned.shape[0] // half
    is_real = lane_is_real((half, width))
    for k in range(freq_count):
        upper = spread[k][:half].astype(jnp.float32)
        lower = spread[k][half:].astype(jnp.float32)
        planes[pl.ds(2 * k, half, stride=terms), :] = jnp.where(
            is_real, upper, pltpu.roll(lower, width // 2, 1)
        )
        planes[pl.ds(2 * k + 1, half, stride=terms), :] = jnp.where(
            is_real, pltpu.roll(upper, width // 2, 1), lower
        )
    limit = cutoff[...]
    sample_index = lax.broadcasted_iota(jnp.int32, (NT // 2, width), 0)
    group = narrow.shape[1] // width

    def per_group(step, _):
        first = pl.multiple_of(step * group, group)
        block = planes[pl.ds(pl.multiple_of(first * terms, terms * group), terms * group), :]
        values = jnp.concatenate([block[r * terms : (r + 1) * terms] for r in range(group)], 1)
        wide[...] = jnp.dot(
            ahead[...], values.astype(jnp.bfloat16), preferred_element_type=jnp.float32
        )
        starts = mute[pl.ds(first, group), :]
        for r in range(group):
            lanes = pl.ds(r * width, width)
            early = wide[: NT // 2, lanes]
            late = wide[NT // 2 :, lanes]
            early = early - jnp.clip(early, -limit, limit)
            early = jnp.where(sample_index >= starts[r : r + 1], early, 0.0)
            late = late - jnp.clip(late, -limit, limit)
            narrow[: NT // 2, lanes] = early.astype(narrow.dtype)
            narrow[NT // 2 :, lanes] = late.astype(narrow.dtype)
        total = jnp.dot(back[...], narrow[...], preferred_element_type=jnp.float32)
        returned[pl.ds(pl.multiple_of(first * sums, sums * group), sums * group), :] = (
            jnp.concatenate([total[:, r * width : (r + 1) * width] for r in range(group)], 0)
        )
        return 0

    lax.fori_loop(0, half // group, per_group, 0)
    for k in range(kept):
        real_part = returned[pl.ds(2 * k, half, stride=sums), :]
        imag_part = returned[pl.ds(2 * k + 1, half, stride=sums), :]
        out[k, :half] = jnp.where(is_real, real_part, pltpu.roll(imag_part, width // 2, 1))
        out[k, half:] = jnp.where(is_real, pltpu.roll(real_part, width // 2, 1), imag_part)


def sparsify(spread, mute, cutoff, ahead, back, kept):
    rows, width = spread[0].shape
    terms, sums = 2 * len(spread), back.shape[0]
    group = math.gcd(rows // 2, 32)
    return pl.pallas_call(
        sparsify_kernel,
        out_shape=jax.ShapeDtypeStruct((kept, rows, width), jnp.float32),
        scratch_shapes=[
            pltpu.VMEM((rows // 2 * terms, width), jnp.float32),
            pltpu.VMEM((rows // 2 * sums, width), jnp.float32),
            pltpu.VMEM((NT, group * width), jnp.float32),
            pltpu.VMEM((NT, group * width), jnp.bfloat16),
        ],
        compiler_params=room(16),
        name="sparsify",
    )(mute, cutoff, ahead, back, *spread)


def wave(shape, sample_dim, freq_count, kept):
    entry = lax.broadcasted_iota(jnp.int32, shape, 1 - sample_dim)
    sample = lax.broadcasted_iota(jnp.int32, shape, sample_dim)
    order = lax.rem(lax.shift_right_logical(entry, 1) + kept * lax.axis_index("freq"), freq_count)
    turns = sample * (order + NT // 4) + (entry & 1) * (NT // 4)
    phases = lax.rem(turns, NT).astype(jnp.float32)
    return jnp.cos(phases * (2.0 * math.pi / NT))


def tables_kernel(kept, freq_count, mute_start, thresholds, mute, cutoff, ahead, back):
    starts = mute_start[...].T
    half = starts.shape[0] // 2
    mute[...] = jnp.concatenate([starts[:half], starts[half:]], 1)
    cutoff[...] = jnp.concatenate([thresholds[...], thresholds[...]], 1)
    ahead[...] = (wave(ahead.shape, 0, freq_count, kept) / math.sqrt(freq_count)).astype(
        ahead.dtype
    )
    scale = 2.0 * math.sqrt(freq_count) / NT
    back[...] = (wave(back.shape, 1, freq_count, kept) * scale).astype(back.dtype)


def tables(mute_start, thresholds, kept, freq_count):
    height, sources = mute_start.shape
    sums = -(-2 * kept // 8) * 8
    return pl.pallas_call(
        functools.partial(tables_kernel, kept, freq_count),
        in_specs=[whole(), whole()],
        out_specs=[whole()] * 4,
        out_shape=[
            jax.ShapeDtypeStruct((height // 2, 2 * sources), jnp.int32),
            jax.ShapeDtypeStruct((1, 2 * sources), jnp.float32),
            jax.ShapeDtypeStruct((NT, 2 * freq_count), jnp.bfloat16),
            jax.ShapeDtypeStruct((sums, NT), jnp.bfloat16),
        ],
        compiler_params=room(4),
        name="tables",
    )(mute_start.T, thresholds[None])


def shuffle(partial_value):
    inside, freqs, slots, columns = partial_value.shape
    tile_count = lax.axis_size("tile")
    group_size = tile_count // inside
    if group_size == 1:
        return lax.all_to_all(partial_value, "tile", split_axis=0, concat_axis=0, tiled=True)
    outgoing = jnp.broadcast_to(
        partial_value[:, None], (inside, group_size, freqs, slots, columns)
    )
    outgoing = outgoing.reshape(tile_count, freqs, slots, columns)
    incoming = lax.all_to_all(outgoing, "tile", split_axis=0, concat_axis=0, tiled=True)
    incoming = incoming.reshape(inside, group_size, freqs, slots, columns).astype(jnp.float32)
    return jnp.sum(incoming, 1).astype(jnp.bfloat16)


def from_others(value):
    size = lax.axis_size("freq")
    return [
        lax.ppermute(value, "freq", [((d + shift) % size, d) for d in range(size)])
        for shift in range(1, size)
    ]


def body(left_basis, right_basis, start_model, recorded, tile_ranks, mute_start, thresholds):
    kept = start_model.shape[0]
    freq_count = kept * lax.axis_size("freq")
    mute, cutoff, ahead, back = tables(mute_start, thresholds, kept, freq_count)
    freqs = range(kept)
    model = start_model
    for outer_step in range(OUTER):
        forward = shuffle(partials(right_basis, model, tile_ranks))
        misfit, outgoing = residual(left_basis, forward, recorded, tile_ranks)
        adjoint = shuffle(outgoing)
        own = [update(right_basis, adjoint, model, f) for f in freqs]
        others = [from_others(value) for value in own]
        spread = own + [others[f][d] for d in range(len(others[0])) for f in freqs]
        model = sparsify(spread, mute, cutoff, ahead, back, kept)
    return (model, misfit)


def solution(mesh):
    return jax.shard_map(
        body,
        mesh=mesh,
        in_specs=(
            P("freq", "tile", None, None),
            P("freq", "tile", None, None),
            P("freq", "tile", None),
            P("freq", "tile", None),
            P(),
            P("tile", None),
            P(),
        ),
        out_specs=(P("freq", "tile", None), P("freq", "tile", None)),
        check_vma=False,
    )
```

time: 217 us -> 168 us (0.77)
  blocking collectives: 0 us -> 98.5 us
  Pallas kernels: 111 us -> 45.8 us
  waiting for transfers between devices: 57.7 us -> 11 us
  starting transfers between devices: 38.7 us -> 4.31 us
    all_to_all x0 -> x4, blocking collectives: none -> 98.5 us  [shuffle(): lax.all_to_all(partial_value, 'tile', split_axis=0, concat_axis=0, tiled=...]
    all_to_all x8 -> x0, waiting for transfers between devices: 52.2 us -> none  [shuffle(): lax.all_to_all(partial_value, 'tile', split_axis=0, concat_axis=0, tiled=...]
    pallas_call x2, Pallas kernels: 54.9 us -> 21.4 us  [sparsify(): pl.pallas_call(sparsify_kernel, out_shape=jax.ShapeDtypeStruct((kept, row...]
    all_to_all x8 -> x0, starting transfers between devices: 32.8 us -> none  [shuffle(): lax.all_to_all(partial_value, 'tile', split_axis=0, concat_axis=0, tiled=...]
    pallas_call x12 -> x9, Pallas kernels: 56.1 us -> 24.4 us  [the longest x2 14.3 us: residual(): pl.pallas_call(residual_kernel, in_specs=[pl.BlockSpec(memory_space=pltpu...]
    ppermute x4, waiting for transfers between devices: 5.51 us -> 11 us  [from_others(): lax.ppermute(value, 'freq', [((d + shift) % size, d) for d in range(size)])]
    unnamed x32 -> x26, local copies, waits for them, and re-layouts: 3.72 us -> 7.35 us
  transfers between devices with their start and end apart: 12 -> 4, of which waited for: 10 -> 4; matrix products, arithmetic and copies ran while one was open for 2% -> 0% of each run, Pallas kernels for 22% -> 2%
where the time goes in v1:
time: 168 us
  blocking collectives  98.5 us (59%)
  Pallas kernels  45.8 us (27%)
  waiting for transfers between devices  11 us (7%)
  local copies, waits for them, and re-layouts  7.35 us (4%)
  starting transfers between devices  4.31 us (3%)
    all_to_all x4, blocking collectives, shuffle(): lax.all_to_all(partial_value, 'tile', split_axis=0, concat_axis=0, tiled=...  98.5 us
    pallas_call x2, Pallas kernels, sparsify(): pl.pallas_call(sparsify_kernel, out_shape=jax.ShapeDtypeStruct((kept, row...  21.4 us
    pallas_call x2, Pallas kernels, residual(): pl.pallas_call(residual_kernel, in_specs=[pl.BlockSpec(memory_space=pltpu...  14.3 us
    ppermute x4, waiting for transfers between devices, from_others(): lax.ppermute(value, 'freq', [((d + shift) % size, d) for d in range(size)])  11 us
    unnamed x26, local copies, waits for them, and re-layouts  7.35 us
    pallas_call x4, Pallas kernels, update(): pl.pallas_call(functools.partial(update_kernel, freq), in_specs=[whole(),...  4.74 us
    pallas_call x2, Pallas kernels, partials(): pl.pallas_call(partials_kernel, in_specs=[pl.BlockSpec(memory_space=pltpu...  4.66 us
    ppermute x4, starting transfers between devices, from_others(): lax.ppermute(value, 'freq', [((d + shift) % size, d) for d in range(size)])  4.31 us
  transfers between devices with their start and end apart: 4, of which 4 were waited for; matrix products, arithmetic and copies ran while one was open for 0% of the time, Pallas kernels for 2%

profile of v1, /device:TPU:0, one launch (start us, length us, event | category | flops | bytes accessed | tf_op | source)
XLA Modules:
  0.0 167.8 jit_solution(5247734044796603488)
XLA Ops:
  0.6 0.0 copy-start
  0.6 2.8 %copy-done = bf16[2,512,2,1536]{3,2,1,0:T(2,128)(2,1)S(1)} copy-done((bf16[2,512,2,1536]{3,2,1,0:T(2,128)(2,1)S(1)}, bf16[2,512,2,1536]{3,2,1,0:T(2,128)(2,1)}, u32[]{:S(2)}) %copy-start) | copy-done | bytes 6291480
  3.4 1.0 copy-done.2
  4.5 0.7 copy-done.5
  5.2 2.3 %partials.2 = bf16[16,2,96,128]{3,2,1,0:T(8,128)(2,1)S(1)} custom-call(s32[16,16]{1,0:T(8,128)S(1)} %copy-done.5, bf16[2,512,2,1536]{3,2,1,0:T(2,128)(2,1)S(1)} %copy-done, f32[2,512,128]{2,1,0:T(8,128)S(1)} %copy-done.2), custom_call_target="tpu_custom_call" | custom-call | tf_op jit(solution)/shard_map/partials/pallas_call | solution.py:82
  7.5 0.0 copy-start.3
  7.5 27.5 %all_to_all.20.coefficient = bf16[16,2,96,128]{3,2,1,0:T(8,128)(2,1)S(1)} all-to-all(bf16[16,2,96,128]{3,2,1,0:T(8,128)(2,1)S(1)} %partials.2), channel_id=1, replica_groups=mesh['freq'=2,'tile'=16] {'tile'}, dimensions={0} | all-to-all | bytes 1572864 | tf_op jit(solution)/shard_map/all_to_all | solution.py:251
  35.0 2.8 %copy-done.1 = bf16[2,512,2,1536]{3,2,1,0:T(2,128)(2,1)S(1)} copy-done((bf16[2,512,2,1536]{3,2,1,0:T(2,128)(2,1)S(1)}, bf16[2,512,2,1536]{3,2,1,0:T(2,128)(2,1)}, u32[]{:S(2)}) %copy-start.1) | copy-done | bytes 6291480
  37.8 7.2 %residual.2 = (f32[2,512,128]{2,1,0:T(8,128)}, bf16[16,2,96,128]{3,2,1,0:T(8,128)(2,1)S(1)}) custom-call(s32[16,16]{1,0:T(8,128)S(1)} %copy-done.5, bf16[2,512,2,1536]{3,2,1,0:T(2,128)(2,1)S(1)} %copy-done.1, bf16[16,2,96,128]{3,2,1,0:T(8,128)(2,1)S(1)} %all_to_all.20.coefficient, f32[2,512,128]{2,1,0:T(8,128)S(1)} %copy-done.4), custom_call_target="tpu_custom_call" | custom-call | tf_op jit(solution)/shard_map/residual/pallas_call | solution.py:104
  44.9 23.8 %all_to_all.21.coefficient = bf16[16,2,96,128]{3,2,1,0:T(8,128)(2,1)S(1)} all-to-all(bf16[16,2,96,128]{3,2,1,0:T(8,128)(2,1)S(1)} %get-tuple-element.13), channel_id=1, replica_groups=mesh['freq'=2,'tile'=16] {'tile'}, dimensions={0} | all-to-all | bytes 1572864 | tf_op jit(solution)/shard_map/all_to_all | solution.py:251
  68.8 0.0 copy-start.7
  68.8 0.0 copy-start.8
  68.8 1.2 update.4.rest_0_
  70.0 1.6 collective-permute-start
  71.6 1.2 update.5.rest_1_
  72.8 0.6 collective-permute-start.1
  73.4 0.7 tables.1
  74.0 2.4 %collective-permute-done.rest_2_ = bf16[512,128]{1,0:T(8,128)(2,1)S(1)} collective-permute-done((bf16[512,128]{1,0:T(8,128)(2,1)S(1)}, bf16[512,128]{1,0:T(8,128)(2,1)S(1)}, u32[]{:S(2)}, u32[]{:S(2)}) %collective-permute-start) | collective-permute-done | bytes 131104 | tf_op jit(solution)/shard_map/ppermute | solution.py:264
  76.4 2.8 %collective-permute-done.1.rest_3_ = bf16[512,128]{1,0:T(8,128)(2,1)S(1)} collective-permute-done((bf16[512,128]{1,0:T(8,128)(2,1)S(1)}, bf16[512,128]{1,0:T(8,128)(2,1)S(1)}, u32[]{:S(2)}, u32[]{:S(2)}) %collective-permute-start.1) | collective-permute-done | bytes 131104 | tf_op jit(solution)/shard_map/ppermute | solution.py:264
  79.2 10.3 %sparsify.2.vector.model = f32[2,512,128]{2,1,0:T(8,128)S(1)} custom-call(s32[256,128]{1,0:T(8,128)S(1)} %get-tuple-element.9.mute, f32[1,128]{1,0:T(1,128)S(1)} %get-tuple-element.10.cutoff, bf16[256,8]{1,0:T(8,128)(2,1)S(1)} %get-tuple-element.11.ahead, bf16[8,256]{1,0:T(8,128)(2,1)S(1)} %get-tuple-element.12.back, bf16[512,128]{1,0:T(8,128)(2,1)S(1)} %update.4.rest_0_, ...), custom_call_target="tpu_custom_call" | custom-call | tf_op jit(solution)/shard_map/sparsify/pallas_call | solution.py:193
  89.5 0.0 slice-start.3
  89.6 2.3 %partials.3 = bf16[16,2,96,128]{3,2,1,0:T(8,128)(2,1)S(1)} custom-call(s32[16,16]{1,0:T(8,128)S(1)} %copy-done.6, bf16[2,512,2,1536]{3,2,1,0:T(2,128)(2,1)S(1)} %bitcast.3, f32[2,512,128]{2,1,0:T(8,128)S(1)} %sparsify.2.vector.model), custom_call_target="tpu_custom_call" | custom-call | tf_op jit(solution)/shard_map/partials/pallas_call | solution.py:82
  91.9 23.3 %all_to_all.22.coefficient = bf16[16,2,96,128]{3,2,1,0:T(8,128)(2,1)S(1)} all-to-all(bf16[16,2,96,128]{3,2,1,0:T(8,128)(2,1)S(1)} %partials.3), channel_id=1, replica_groups=mesh['freq'=2,'tile'=16] {'tile'}, dimensions={0} | all-to-all | bytes 1572864 | tf_op jit(solution)/shard_map/all_to_all | solution.py:251
  115.2 7.2 %residual.3 = (f32[2,512,128]{2,1,0:T(8,128)}, bf16[16,2,96,128]{3,2,1,0:T(8,128)(2,1)S(1)}) custom-call(s32[16,16]{1,0:T(8,128)S(1)} %copy-done.6, bf16[2,512,2,1536]{3,2,1,0:T(2,128)(2,1)S(1)} %bitcast.5, bf16[16,2,96,128]{3,2,1,0:T(8,128)(2,1)S(1)} %all_to_all.22.coefficient, f32[2,512,128]{2,1,0:T(8,128)S(1)} %copy-done.4), custom_call_target="tpu_custom_call" | custom-call | tf_op jit(solution)/shard_map/residual/pallas_call | solution.py:104
  122.4 23.8 %all_to_all.23.coefficient = bf16[16,2,96,128]{3,2,1,0:T(8,128)(2,1)S(1)} all-to-all(bf16[16,2,96,128]{3,2,1,0:T(8,128)(2,1)S(1)} %get-tuple-element.14), channel_id=1, replica_groups=mesh['freq'=2,'tile'=16] {'tile'}, dimensions={0} | all-to-all | bytes 1572864 | tf_op jit(solution)/shard_map/all_to_all | solution.py:251
  146.2 1.2 update.6.rest_0_
  147.4 1.6 collective-permute-start.2
  149.0 1.2 update.7.rest_1_
  150.2 0.6 collective-permute-start.3
  150.8 3.1 %collective-permute-done.2.rest_2_ = bf16[512,128]{1,0:T(8,128)(2,1)S(1)} collective-permute-done((bf16[512,128]{1,0:T(8,128)(2,1)S(1)}, bf16[512,128]{1,0:T(8,128)(2,1)S(1)}, u32[]{:S(2)}, u32[]{:S(2)}) %collective-permute-start.2) | collective-permute-done | bytes 131104 | tf_op jit(solution)/shard_map/ppermute | solution.py:264
  153.9 2.8 %collective-permute-done.3.rest_3_ = bf16[512,128]{1,0:T(8,128)(2,1)S(1)} collective-permute-done((bf16[512,128]{1,0:T(8,128)(2,1)S(1)}, bf16[512,128]{1,0:T(8,128)(2,1)S(1)}, u32[]{:S(2)}, u32[]{:S(2)}) %collective-permute-start.3) | collective-permute-done | bytes 131104 | tf_op jit(solution)/shard_map/ppermute | solution.py:264
  156.6 11.1 %sparsify.3 = f32[2,512,128]{2,1,0:T(8,128)} custom-call(s32[256,128]{1,0:T(8,128)S(1)} %get-tuple-element.9.mute, f32[1,128]{1,0:T(1,128)S(1)} %get-tuple-element.10.cutoff, bf16[256,8]{1,0:T(8,128)(2,1)S(1)} %get-tuple-element.11.ahead, bf16[8,256]{1,0:T(8,128)(2,1)S(1)} %get-tuple-element.12.back, bf16[512,128]{1,0:T(8,128)(2,1)S(1)} %update.6.rest_0_, ...), custom_call_target="tpu_custom_call" | custom-call | tf_op jit(solution)/shard_map/sparsify/pallas_call | solution.py:193
  (19 shorter events, 0.0 us)
Async XLA Ops:
  0.6 2.8 %copy-start = (bf16[2,512,2,1536]{3,2,1,0:T(2,128)(2,1)S(1)}, bf16[2,512,2,1536]{3,2,1,0:T(2,128)(2,1)}, u32[]{:S(2)}) copy-start(bf16[2,512,2,1536]{3,2,1,0:T(2,128)(2,1)} %basis.15) | copy-start | bytes 18874372
  3.4 1.0 copy-start.2
  4.5 0.7 copy-start.5
  5.2 29.8 %copy-start.4 = (f32[2,512,128]{2,1,0:T(8,128)S(1)}, f32[2,512,128]{2,1,0:T(8,128)}, u32[]{:S(2)}) copy-start(f32[2,512,128]{2,1,0:T(8,128)} %recorded.3) | copy-start | bytes 1572868
  5.2 63.6 %slice-start = ((s8[6291456]{0:T(1024)(128)(4,1)}), s8[4194304]{0:T(1024)(128)(4,1)S(1)}, s32[]{:S(2)}) async-start(s8[6291456]{0:T(1024)(128)(4,1)} %bitcast.2), calls=%async_computation.4 | async-start | bytes 8388608
  7.5 61.3 %copy-start.3 = (f32[2,512,128]{2,1,0:T(8,128)S(1)}, f32[2,512,128]{2,1,0:T(8,128)}, u32[]{:S(2)}) copy-start(f32[2,512,128]{2,1,0:T(8,128)} %model.3) | copy-start | bytes 1572868
  35.0 2.8 %copy-start.1 = (bf16[2,512,2,1536]{3,2,1,0:T(2,128)(2,1)S(1)}, bf16[2,512,2,1536]{3,2,1,0:T(2,128)(2,1)}, u32[]{:S(2)}) copy-start(bf16[2,512,2,1536]{3,2,1,0:T(2,128)(2,1)} %basis.13) | copy-start | bytes 18874372
  37.8 31.0 %slice-start.1 = ((s8[6291456]{0:T(1024)(128)(4,1)}), s8[2097152]{0:T(1024)(128)(4,1)S(1)}, s32[]{:S(2)}) async-start(s8[6291456]{0:T(1024)(128)(4,1)} %bitcast.2), calls=%async_computation.5 | async-start | bytes 4194304
  68.8 4.6 %copy-start.7 = (s32[512,64]{0,1:T(8,128)S(1)}, s32[512,64]{0,1:T(8,128)}, u32[]{:S(2)}) copy-start(s32[512,64]{0,1:T(8,128)} %param.12) | copy-start | bytes 393220
  68.8 4.6 %copy-start.8 = (f32[64]{0:T(128)S(1)}, f32[64]{0:T(128)}, u32[]{:S(2)}) copy-start(f32[64]{0:T(128)} %param.13) | copy-start | bytes 772
  70.0 19.5 %copy-start.6 = (s32[16,16]{1,0:T(8,128)S(1)}, s32[16,16]{1,0:T(8,128)}, u32[]{:S(2)}) copy-start(s32[16,16]{1,0:T(8,128)} %ranks.7) | copy-start | bytes 3076
  70.0 6.4 %collective-permute-start = (bf16[512,128]{1,0:T(8,128)(2,1)S(1)}, bf16[512,128]{1,0:T(8,128)(2,1)S(1)}, u32[]{:S(2)}, u32[]{:S(2)}) collective-permute-start(bf16[512,128]{1,0:T(8,128)(2,1)S(1)} %update.4.rest_0_), channel_id=1, source_target_pairs={{16,0},{0,16},{17,1},{1,17},{18,2},{2,18},{19,3},{3,19},{20,4},{4,... | collective-permute-start | bytes 393224 | tf_op jit(solution)/shard_map/ppermute | solution.py:264
  71.6 43.7 %slice-start.2 = ((s8[6291456]{0:T(1024)(128)(4,1)}), s8[4194304]{0:T(1024)(128)(4,1)S(1)}, s32[]{:S(2)}) async-start(s8[6291456]{0:T(1024)(128)(4,1)} %bitcast.4), calls=%async_computation.6 | async-start | bytes 8388608
  72.8 6.4 %collective-permute-start.1 = (bf16[512,128]{1,0:T(8,128)(2,1)S(1)}, bf16[512,128]{1,0:T(8,128)(2,1)S(1)}, u32[]{:S(2)}, u32[]{:S(2)}) collective-permute-start(bf16[512,128]{1,0:T(8,128)(2,1)S(1)} %update.5.rest_1_), channel_id=1, source_target_pairs={{16,0},{0,16},{17,1},{1,17},{18,2},{2,18},{19,3},{3,19},{20,4},{4,... | collective-permute-start | bytes 393224 | tf_op jit(solution)/shard_map/ppermute | solution.py:264
  89.5 25.7 %slice-start.3 = ((s8[6291456]{0:T(1024)(128)(4,1)}), s8[2097152]{0:T(1024)(128)(4,1)S(1)}, s32[]{:S(2)}) async-start(s8[6291456]{0:T(1024)(128)(4,1)} %bitcast.4), calls=%async_computation.7 | async-start | bytes 4194304
  147.4 6.4 %collective-permute-start.2 = (bf16[512,128]{1,0:T(8,128)(2,1)S(1)}, bf16[512,128]{1,0:T(8,128)(2,1)S(1)}, u32[]{:S(2)}, u32[]{:S(2)}) collective-permute-start(bf16[512,128]{1,0:T(8,128)(2,1)S(1)} %update.6.rest_0_), channel_id=1, source_target_pairs={{16,0},{0,16},{17,1},{1,17},{18,2},{2,18},{19,3},{3,19},{20,4},{4,... | collective-permute-start | bytes 393224 | tf_op jit(solution)/shard_map/ppermute | solution.py:264
  150.2 6.4 %collective-permute-start.3 = (bf16[512,128]{1,0:T(8,128)(2,1)S(1)}, bf16[512,128]{1,0:T(8,128)(2,1)S(1)}, u32[]{:S(2)}, u32[]{:S(2)}) collective-permute-start(bf16[512,128]{1,0:T(8,128)(2,1)S(1)} %update.7.rest_1_), channel_id=1, source_target_pairs={{16,0},{0,16},{17,1},{1,17},{18,2},{2,18},{19,3},{3,19},{20,4},{4,... | collective-permute-start | bytes 393224 | tf_op jit(solution)/shard_map/ppermute | solution.py:264

commit v2 on v1

--- a/solution.py
+++ b/solution.py
@@ -70,46 +70,87 @@
         out[tile] = jnp.where(level < rank_of(tile), piece, 0.0).astype(out.dtype)
 
 
-def partials_kernel(ranks, basis, vector, out, pairs):
+def partials_kernel(ranks, basis, vector, out, *pairs):
     block = block_of(ranks.shape[0])
     for f in range(basis.shape[0]):
-        contract(basis[f], vector[f], pairs, lambda tile: ranks[tile, block], out.at[:, f])
-
-
-def partials(basis, vector, ranks):
+        contract(basis[f], vector[f], pairs[f], lambda tile: ranks[tile, block], out.at[:, f])
+
+
+def first_partials_kernel(
+    ranks_from, basis_from, vector_from, out, ranks, basis, vector, rank_copied, copied, *pairs
+):
+    freqs = basis.shape[0]
+    ranks_copy = pltpu.make_async_copy(ranks_from, ranks, rank_copied)
+    copies = [
+        [
+            pltpu.make_async_copy(vector_from.at[f], vector.at[f], copied.at[0, f]),
+            pltpu.make_async_copy(basis_from.at[f], basis.at[f], copied.at[1, f]),
+        ]
+        for f in range(freqs)
+    ]
+    for copy in [ranks_copy] + sum(copies, []):
+        copy.start()
+    ranks_copy.wait()
+    block = block_of(ranks.shape[0])
+    for f in range(freqs):
+        for copy in copies[f]:
+            copy.wait()
+        contract(basis[f], vector[f], pairs[f], lambda tile: ranks[tile, block], out.at[:, f])
+
+
+def partials(basis, vector, ranks, first):
     freqs, height, planes, columns = basis.shape
     inside, width = ranks.shape[0], vector.shape[2]
-    return pl.pallas_call(
-        partials_kernel,
-        in_specs=[pl.BlockSpec(memory_space=pltpu.SMEM), whole(), whole()],
+    scratch = [pltpu.VMEM((height * planes, width), jnp.float32)] * freqs
+    if first:
+        in_specs = [pl.BlockSpec(memory_space=pl.ANY)] * 3
+        scratch = [
+            pltpu.SMEM(ranks.shape, ranks.dtype),
+            pltpu.VMEM(basis.shape, basis.dtype),
+            pltpu.VMEM(vector.shape, vector.dtype),
+            pltpu.SemaphoreType.DMA,
+            pltpu.SemaphoreType.DMA((2, freqs)),
+        ] + scratch
+    else:
+        in_specs = [pl.BlockSpec(memory_space=pltpu.SMEM), whole(), whole()]
+    return pl.pallas_call(
+        first_partials_kernel if first else partials_kernel,
+        in_specs=in_specs,
         out_specs=whole(),
         out_shape=jax.ShapeDtypeStruct((inside, freqs, columns // inside, width), jnp.bfloat16),
-        scratch_shapes=[pltpu.VMEM((height * planes, width), jnp.float32)],
-        compiler_params=room(12),
+        scratch_shapes=scratch,
+        compiler_params=room(60 if first else 12),
         name="partials",
     )(ranks, basis, vector)
 
 
-def residual_kernel(ranks, basis, coefficient, recorded, misfit, out, product, pairs):
+def residual_kernel(ranks, basis, coefficient, recorded, *rest):
+    freqs = basis.shape[0]
+    misfit, out, scratch = rest[: -1 - 2 * freqs], rest[-1 - 2 * freqs], rest[-2 * freqs :]
     block = block_of(ranks.shape[0])
-    for f in range(basis.shape[0]):
-        value = expand(basis[f], coefficient[:, f], product) - recorded[f]
-        misfit[f] = value
-        contract(basis[f], value, pairs, lambda tile: ranks[block, tile], out.at[:, f])
-
-
-def residual(basis, coefficient, recorded, ranks):
-    _, height, planes, _ = basis.shape
+    values = []
+    for f in range(freqs):
+        values.append(expand(basis[f], coefficient[:, f], scratch[f]) - recorded[f])
+        if misfit:
+            misfit[0][f] = values[f]
+    for f in range(freqs):
+        contract(
+            basis[f], values[f], scratch[freqs + f], lambda tile: ranks[block, tile], out.at[:, f]
+        )
+
+
+def residual(basis, coefficient, recorded, ranks, last):
+    freqs, height, planes, _ = basis.shape
     scratch = pltpu.VMEM((height * planes, recorded.shape[2]), jnp.float32)
+    out_shape = [jax.ShapeDtypeStruct(coefficient.shape, jnp.bfloat16)]
+    if last:
+        out_shape.insert(0, jax.ShapeDtypeStruct(recorded.shape, jnp.float32))
     return pl.pallas_call(
         residual_kernel,
         in_specs=[pl.BlockSpec(memory_space=pltpu.SMEM), whole(), whole(), whole()],
-        out_specs=[whole(), whole()],
-        out_shape=[
-            jax.ShapeDtypeStruct(recorded.shape, jnp.float32),
-            jax.ShapeDtypeStruct(coefficient.shape, jnp.bfloat16),
-        ],
-        scratch_shapes=[scratch, scratch],
+        out_specs=[whole()] * len(out_shape),
+        out_shape=out_shape,
+        scratch_shapes=[scratch] * (2 * freqs),
         compiler_params=room(12),
         name="residual",
     )(ranks, basis, coefficient, recorded)
@@ -273,14 +314,16 @@
     freqs = range(kept)
     model = start_model
     for outer_step in range(OUTER):
-        forward = shuffle(partials(right_basis, model, tile_ranks))
-        misfit, outgoing = residual(left_basis, forward, recorded, tile_ranks)
+        forward = shuffle(partials(right_basis, model, tile_ranks, outer_step == 0))
+        *misfit, outgoing = residual(
+            left_basis, forward, recorded, tile_ranks, outer_step == OUTER - 1
+        )
         adjoint = shuffle(outgoing)
         own = [update(right_basis, adjoint, model, f) for f in freqs]
         others = [from_others(value) for value in own]
         spread = own + [others[f][d] for d in range(len(others[0])) for f in freqs]
         model = sparsify(spread, mute, cutoff, ahead, back, kept)
-    return (model, misfit)
+    return (model, misfit[0])
 
 
 def solution(mesh):

time: 168 us -> 161 us (0.958)
  local copies, waits for them, and re-layouts: 7.35 us -> 2.83 us
  Pallas kernels: 45.8 us -> 43.3 us
    pallas_call x2, Pallas kernels: 14.3 us -> 9.25 us  [residual(): pl.pallas_call(residual_kernel, in_specs=[pl.BlockSpec(memory_space=pltpu...]
    unnamed x26 -> x20, local copies, waits for them, and re-layouts: 7.35 us -> 2.83 us
    pallas_call x2, Pallas kernels: 4.66 us -> 7.25 us  [partials(): pl.pallas_call(first_partials_kernel if first else partials_kernel, in_sp...]
where the time goes in v2:
time: 161 us
  blocking collectives  98.8 us (61%)
  Pallas kernels  43.3 us (27%)
  waiting for transfers between devices  11 us (7%)
  starting transfers between devices  4.31 us (3%)
  local copies, waits for them, and re-layouts  2.83 us (2%)
    all_to_all x4, blocking collectives, shuffle(): lax.all_to_all(partial_value, 'tile', split_axis=0, concat_axis=0, tiled=...  98.8 us
    pallas_call x2, Pallas kernels, sparsify(): pl.pallas_call(sparsify_kernel, out_shape=jax.ShapeDtypeStruct((kept, row...  21.4 us
    ppermute x4, waiting for transfers between devices, from_others(): lax.ppermute(value, 'freq', [((d + shift) % size, d) for d in range(size)])  11 us
    pallas_call x2, Pallas kernels, residual(): pl.pallas_call(residual_kernel, in_specs=[pl.BlockSpec(memory_space=pltpu...  9.25 us
    pallas_call x2, Pallas kernels, partials(): pl.pallas_call(first_partials_kernel if first else partials_kernel, in_sp...  7.25 us
    pallas_call x4, Pallas kernels, update(): pl.pallas_call(functools.partial(update_kernel, freq), in_specs=[whole(),...  4.73 us
    ppermute x4, starting transfers between devices, from_others(): lax.ppermute(value, 'freq', [((d + shift) % size, d) for d in range(size)])  4.31 us
  transfers between devices with their start and end apart: 4, of which 4 were waited for; matrix products, arithmetic and copies ran while one was open for 0% of the time, Pallas kernels for 2%

profile of v2, /device:TPU:0, one launch (start us, length us, event | category | flops | bytes accessed | tf_op | source)
XLA Modules:
  0.0 161.1 jit_solution(9361164400071210321)
XLA Ops:
  0.6 0.0 copy-start.3
  0.6 0.0 copy-start.2
  0.6 4.9 %partials.2 = bf16[16,2,96,128]{3,2,1,0:T(8,128)(2,1)} custom-call(s32[16,16]{1,0:T(8,128)} %ranks.5, bf16[2,512,2,1536]{3,2,1,0:T(2,128)(2,1)} %basis.13, f32[2,512,128]{2,1,0:T(8,128)} %model.3), custom_call_target="tpu_custom_call" | custom-call | tf_op jit(solution)/shard_map/partials/pallas_call | solution.py:116
  5.6 0.0 slice-start
  5.6 27.8 %all_to_all.20.coefficient = bf16[16,2,96,128]{3,2,1,0:T(8,128)(2,1)S(1)} all-to-all(bf16[16,2,96,128]{3,2,1,0:T(8,128)(2,1)} %partials.2), channel_id=1, replica_groups=mesh['freq'=2,'tile'=16] {'tile'}, dimensions={0} | all-to-all | bytes 1572864 | tf_op jit(solution)/shard_map/all_to_all | solution.py:292
  33.4 0.0 copy-done.2
  33.4 2.8 %copy-done = bf16[2,512,2,1536]{3,2,1,0:T(2,128)(2,1)S(1)} copy-done((bf16[2,512,2,1536]{3,2,1,0:T(2,128)(2,1)S(1)}, bf16[2,512,2,1536]{3,2,1,0:T(2,128)(2,1)}, u32[]{:S(2)}) %copy-start) | copy-done | bytes 6291480
  36.2 4.3 %residual.2 = bf16[16,2,96,128]{3,2,1,0:T(8,128)(2,1)S(1)} custom-call(s32[16,16]{1,0:T(8,128)S(1)} %copy-done.3, bf16[2,512,2,1536]{3,2,1,0:T(2,128)(2,1)S(1)} %copy-done, bf16[16,2,96,128]{3,2,1,0:T(8,128)(2,1)S(1)} %all_to_all.20.coefficient, f32[2,512,128]{2,1,0:T(8,128)S(1)} %copy-done.2), custom_call_target="tpu_custom_call" | custom-call | tf_op jit(solution)/shard_map/residual/pallas_call | solution.py:148
  40.5 23.9 %all_to_all.21.coefficient = bf16[16,2,96,128]{3,2,1,0:T(8,128)(2,1)S(1)} all-to-all(bf16[16,2,96,128]{3,2,1,0:T(8,128)(2,1)S(1)} %residual.2), channel_id=1, replica_groups=mesh['freq'=2,'tile'=16] {'tile'}, dimensions={0} | all-to-all | bytes 1572864 | tf_op jit(solution)/shard_map/all_to_all | solution.py:292
  64.4 0.0 slice-done
  64.4 0.0 copy-start.4
  64.4 0.0 copy-start.5
  64.4 1.2 update.4.rest_0_
  65.6 1.6 collective-permute-start
  67.2 1.2 update.5.rest_1_
  68.4 0.6 collective-permute-start.1
  69.0 0.7 tables.1
  69.6 2.4 %collective-permute-done.rest_2_ = bf16[512,128]{1,0:T(8,128)(2,1)S(1)} collective-permute-done((bf16[512,128]{1,0:T(8,128)(2,1)S(1)}, bf16[512,128]{1,0:T(8,128)(2,1)S(1)}, u32[]{:S(2)}, u32[]{:S(2)}) %collective-permute-start) | collective-permute-done | bytes 131104 | tf_op jit(solution)/shard_map/ppermute | solution.py:305
  72.0 2.8 %collective-permute-done.1.rest_3_ = bf16[512,128]{1,0:T(8,128)(2,1)S(1)} collective-permute-done((bf16[512,128]{1,0:T(8,128)(2,1)S(1)}, bf16[512,128]{1,0:T(8,128)(2,1)S(1)}, u32[]{:S(2)}, u32[]{:S(2)}) %collective-permute-start.1) | collective-permute-done | bytes 131104 | tf_op jit(solution)/shard_map/ppermute | solution.py:305
  74.8 10.3 %sparsify.2.vector.model = f32[2,512,128]{2,1,0:T(8,128)S(1)} custom-call(s32[256,128]{1,0:T(8,128)S(1)} %get-tuple-element.8.mute, f32[1,128]{1,0:T(1,128)S(1)} %get-tuple-element.9.cutoff, bf16[256,8]{1,0:T(8,128)(2,1)S(1)} %get-tuple-element.10.ahead, bf16[8,256]{1,0:T(8,128)(2,1)S(1)} %get-tuple-element.11.back, bf16[512,128]{1,0:T(8,128)(2,1)S(1)} %update.4.rest_0_, ...), custom_call_target="tpu_custom_call" | custom-call | tf_op jit(solution)/shard_map/sparsify/pallas_call | solution.py:234
  85.1 0.0 slice-start.3
  85.1 2.3 %partials.3 = bf16[16,2,96,128]{3,2,1,0:T(8,128)(2,1)S(1)} custom-call(s32[16,16]{1,0:T(8,128)S(1)} %copy-done.3, bf16[2,512,2,1536]{3,2,1,0:T(2,128)(2,1)S(1)} %bitcast.3, f32[2,512,128]{2,1,0:T(8,128)S(1)} %sparsify.2.vector.model), custom_call_target="tpu_custom_call" | custom-call | tf_op jit(solution)/shard_map/partials/pallas_call | solution.py:116
  87.5 23.3 %all_to_all.22.coefficient = bf16[16,2,96,128]{3,2,1,0:T(8,128)(2,1)S(1)} all-to-all(bf16[16,2,96,128]{3,2,1,0:T(8,128)(2,1)S(1)} %partials.3), channel_id=1, replica_groups=mesh['freq'=2,'tile'=16] {'tile'}, dimensions={0} | all-to-all | bytes 1572864 | tf_op jit(solution)/shard_map/all_to_all | solution.py:292
  110.8 4.9 %residual.3 = (f32[2,512,128]{2,1,0:T(8,128)}, bf16[16,2,96,128]{3,2,1,0:T(8,128)(2,1)S(1)}) custom-call(s32[16,16]{1,0:T(8,128)S(1)} %copy-done.3, bf16[2,512,2,1536]{3,2,1,0:T(2,128)(2,1)S(1)} %bitcast.5, bf16[16,2,96,128]{3,2,1,0:T(8,128)(2,1)S(1)} %all_to_all.22.coefficient, f32[2,512,128]{2,1,0:T(8,128)S(1)} %copy-done.2), custom_call_target="tpu_custom_call" | custom-call | tf_op jit(solution)/shard_map/residual/pallas_call | solution.py:148
  115.7 23.8 %all_to_all.23.coefficient = bf16[16,2,96,128]{3,2,1,0:T(8,128)(2,1)S(1)} all-to-all(bf16[16,2,96,128]{3,2,1,0:T(8,128)(2,1)S(1)} %get-tuple-element.12), channel_id=1, replica_groups=mesh['freq'=2,'tile'=16] {'tile'}, dimensions={0} | all-to-all | bytes 1572864 | tf_op jit(solution)/shard_map/all_to_all | solution.py:292
  139.6 1.2 update.6.rest_0_
  140.8 1.6 collective-permute-start.2
  142.3 1.2 update.7.rest_1_
  143.5 0.6 collective-permute-start.3
  144.1 3.1 %collective-permute-done.2.rest_2_ = bf16[512,128]{1,0:T(8,128)(2,1)S(1)} collective-permute-done((bf16[512,128]{1,0:T(8,128)(2,1)S(1)}, bf16[512,128]{1,0:T(8,128)(2,1)S(1)}, u32[]{:S(2)}, u32[]{:S(2)}) %collective-permute-start.2) | collective-permute-done | bytes 131104 | tf_op jit(solution)/shard_map/ppermute | solution.py:305
  147.2 2.8 %collective-permute-done.3.rest_3_ = bf16[512,128]{1,0:T(8,128)(2,1)S(1)} collective-permute-done((bf16[512,128]{1,0:T(8,128)(2,1)S(1)}, bf16[512,128]{1,0:T(8,128)(2,1)S(1)}, u32[]{:S(2)}, u32[]{:S(2)}) %collective-permute-start.3) | collective-permute-done | bytes 131104 | tf_op jit(solution)/shard_map/ppermute | solution.py:305
  150.0 11.1 %sparsify.3 = f32[2,512,128]{2,1,0:T(8,128)} custom-call(s32[256,128]{1,0:T(8,128)S(1)} %get-tuple-element.8.mute, f32[1,128]{1,0:T(1,128)S(1)} %get-tuple-element.9.cutoff, bf16[256,8]{1,0:T(8,128)(2,1)S(1)} %get-tuple-element.10.ahead, bf16[8,256]{1,0:T(8,128)(2,1)S(1)} %get-tuple-element.11.back, bf16[512,128]{1,0:T(8,128)(2,1)S(1)} %update.6.rest_0_, ...), custom_call_target="tpu_custom_call" | custom-call | tf_op jit(solution)/shard_map/sparsify/pallas_call | solution.py:234
  (13 shorter events, 0.0 us)
Async XLA Ops:
  0.6 32.8 %copy-start.3 = (s32[16,16]{1,0:T(8,128)S(1)}, s32[16,16]{1,0:T(8,128)}, u32[]{:S(2)}) copy-start(s32[16,16]{1,0:T(8,128)} %ranks.5) | copy-start | bytes 3076
  0.6 32.8 %copy-start.2 = (f32[2,512,128]{2,1,0:T(8,128)S(1)}, f32[2,512,128]{2,1,0:T(8,128)}, u32[]{:S(2)}) copy-start(f32[2,512,128]{2,1,0:T(8,128)} %recorded.3) | copy-start | bytes 1572868
  5.6 58.8 %slice-start = ((s8[6291456]{0:T(1024)(128)(4,1)}), s8[4194304]{0:T(1024)(128)(4,1)S(1)}, s32[]{:S(2)}) async-start(s8[6291456]{0:T(1024)(128)(4,1)} %bitcast.2), calls=%async_computation.4 | async-start | bytes 8388608
  33.4 2.8 %copy-start = (bf16[2,512,2,1536]{3,2,1,0:T(2,128)(2,1)S(1)}, bf16[2,512,2,1536]{3,2,1,0:T(2,128)(2,1)}, u32[]{:S(2)}) copy-start(bf16[2,512,2,1536]{3,2,1,0:T(2,128)(2,1)} %basis.11) | copy-start | bytes 18874372
  36.2 28.2 %slice-start.1 = ((s8[6291456]{0:T(1024)(128)(4,1)}), s8[2097152]{0:T(1024)(128)(4,1)S(1)}, s32[]{:S(2)}) async-start(s8[6291456]{0:T(1024)(128)(4,1)} %bitcast.2), calls=%async_computation.5 | async-start | bytes 4194304
  36.2 28.2 %copy-start.1 = (f32[2,512,128]{2,1,0:T(8,128)S(1)}, f32[2,512,128]{2,1,0:T(8,128)}, u32[]{:S(2)}) copy-start(f32[2,512,128]{2,1,0:T(8,128)} %model.3) | copy-start | bytes 1572868
  64.4 4.6 %copy-start.4 = (s32[512,64]{0,1:T(8,128)S(1)}, s32[512,64]{0,1:T(8,128)}, u32[]{:S(2)}) copy-start(s32[512,64]{0,1:T(8,128)} %param.12) | copy-start | bytes 393220
  64.4 4.6 %copy-start.5 = (f32[64]{0:T(128)S(1)}, f32[64]{0:T(128)}, u32[]{:S(2)}) copy-start(f32[64]{0:T(128)} %param.13) | copy-start | bytes 772
  65.6 6.4 %collective-permute-start = (bf16[512,128]{1,0:T(8,128)(2,1)S(1)}, bf16[512,128]{1,0:T(8,128)(2,1)S(1)}, u32[]{:S(2)}, u32[]{:S(2)}) collective-permute-start(bf16[512,128]{1,0:T(8,128)(2,1)S(1)} %update.4.rest_0_), channel_id=1, source_target_pairs={{16,0},{0,16},{17,1},{1,17},{18,2},{2,18},{19,3},{3,19},{20,4},{4,... | collective-permute-start | bytes 393224 | tf_op jit(solution)/shard_map/ppermute | solution.py:305
  67.2 43.7 %slice-start.2 = ((s8[6291456]{0:T(1024)(128)(4,1)}), s8[4194304]{0:T(1024)(128)(4,1)S(1)}, s32[]{:S(2)}) async-start(s8[6291456]{0:T(1024)(128)(4,1)} %bitcast.4), calls=%async_computation.6 | async-start | bytes 8388608
  68.4 6.4 %collective-permute-start.1 = (bf16[512,128]{1,0:T(8,128)(2,1)S(1)}, bf16[512,128]{1,0:T(8,128)(2,1)S(1)}, u32[]{:S(2)}, u32[]{:S(2)}) collective-permute-start(bf16[512,128]{1,0:T(8,128)(2,1)S(1)} %update.5.rest_1_), channel_id=1, source_target_pairs={{16,0},{0,16},{17,1},{1,17},{18,2},{2,18},{19,3},{3,19},{20,4},{4,... | collective-permute-start | bytes 393224 | tf_op jit(solution)/shard_map/ppermute | solution.py:305
  85.1 25.7 %slice-start.3 = ((s8[6291456]{0:T(1024)(128)(4,1)}), s8[2097152]{0:T(1024)(128)(4,1)S(1)}, s32[]{:S(2)}) async-start(s8[6291456]{0:T(1024)(128)(4,1)} %bitcast.4), calls=%async_computation.7 | async-start | bytes 4194304
  140.8 6.4 %collective-permute-start.2 = (bf16[512,128]{1,0:T(8,128)(2,1)S(1)}, bf16[512,128]{1,0:T(8,128)(2,1)S(1)}, u32[]{:S(2)}, u32[]{:S(2)}) collective-permute-start(bf16[512,128]{1,0:T(8,128)(2,1)S(1)} %update.6.rest_0_), channel_id=1, source_target_pairs={{16,0},{0,16},{17,1},{1,17},{18,2},{2,18},{19,3},{3,19},{20,4},{4,... | collective-permute-start | bytes 393224 | tf_op jit(solution)/shard_map/ppermute | solution.py:305
  143.5 6.5 %collective-permute-start.3 = (bf16[512,128]{1,0:T(8,128)(2,1)S(1)}, bf16[512,128]{1,0:T(8,128)(2,1)S(1)}, u32[]{:S(2)}, u32[]{:S(2)}) collective-permute-start(bf16[512,128]{1,0:T(8,128)(2,1)S(1)} %update.7.rest_1_), channel_id=1, source_target_pairs={{16,0},{0,16},{17,1},{1,17},{18,2},{2,18},{19,3},{3,19},{20,4},{4,... | collective-permute-start | bytes 393224 | tf_op jit(solution)/shard_map/ppermute | solution.py:305

commit v3 on v2

--- a/solution.py
+++ b/solution.py
@@ -11,6 +11,7 @@
 NT = 256
 OUTER = 2
 STEP_SIZE = 0.5
+PIECES = 2
 
 
 def lane_is_real(shape):
@@ -70,10 +71,13 @@
         out[tile] = jnp.where(level < rank_of(tile), piece, 0.0).astype(out.dtype)
 
 
-def partials_kernel(ranks, basis, vector, out, *pairs):
+def partials_kernel(ranks, basis, *rest):
+    freqs = basis.shape[0]
+    pieces, out, pairs = rest[: -1 - freqs], rest[-1 - freqs], rest[-freqs:]
     block = block_of(ranks.shape[0])
-    for f in range(basis.shape[0]):
-        contract(basis[f], vector[f], pairs[f], lambda tile: ranks[tile, block], out.at[:, f])
+    for f in range(freqs):
+        vector = jnp.concatenate([piece[f] for piece in pieces], 0)
+        contract(basis[f], vector, pairs[f], lambda tile: ranks[tile, block], out.at[:, f])
 
 
 def first_partials_kernel(
@@ -98,21 +102,21 @@
         contract(basis[f], vector[f], pairs[f], lambda tile: ranks[tile, block], out.at[:, f])
 
 
-def partials(basis, vector, ranks, first):
+def partials(basis, pieces, ranks, first):
     freqs, height, planes, columns = basis.shape
-    inside, width = ranks.shape[0], vector.shape[2]
+    inside, width = ranks.shape[0], pieces[0].shape[2]
     scratch = [pltpu.VMEM((height * planes, width), jnp.float32)] * freqs
     if first:
         in_specs = [pl.BlockSpec(memory_space=pl.ANY)] * 3
         scratch = [
             pltpu.SMEM(ranks.shape, ranks.dtype),
             pltpu.VMEM(basis.shape, basis.dtype),
-            pltpu.VMEM(vector.shape, vector.dtype),
+            pltpu.VMEM(pieces[0].shape, pieces[0].dtype),
             pltpu.SemaphoreType.DMA,
             pltpu.SemaphoreType.DMA((2, freqs)),
         ] + scratch
     else:
-        in_specs = [pl.BlockSpec(memory_space=pltpu.SMEM), whole(), whole()]
+        in_specs = [pl.BlockSpec(memory_space=pltpu.SMEM), whole()] + [whole()] * len(pieces)
     return pl.pallas_call(
         first_partials_kernel if first else partials_kernel,
         in_specs=in_specs,
@@ -121,7 +125,7 @@
         scratch_shapes=scratch,
         compiler_params=room(60 if first else 12),
         name="partials",
-    )(ranks, basis, vector)
+    )(ranks, basis, *pieces)
 
 
 def residual_kernel(ranks, basis, coefficient, recorded, *rest):
@@ -156,31 +160,34 @@
     )(ranks, basis, coefficient, recorded)
 
 
-def update_kernel(freq, basis, coefficient, model, out, product):
-    gradient = expand(basis[freq], coefficient[:, freq], product)
-    out[...] = (model[freq] - STEP_SIZE * gradient).astype(out.dtype)
-
-
-def update(basis, coefficient, model, freq):
-    _, height, planes, _ = basis.shape
+def update_kernel(first_row, model_row, basis, coefficient, model, out, *scratch):
+    freqs, rows, _ = out.shape
+    for f in range(freqs):
+        part = basis[f, first_row : first_row + rows]
+        gradient = expand(part, coefficient[:, f], scratch[f])
+        before = model[f, model_row : model_row + rows]
+        out[f] = (before - STEP_SIZE * gradient).astype(out.dtype)
+
+
+def update(basis, coefficient, model, first_row, rows, model_row):
+    freqs, _, planes, _ = basis.shape
     width = model.shape[2]
     return pl.pallas_call(
-        functools.partial(update_kernel, freq),
+        functools.partial(update_kernel, first_row, model_row),
         in_specs=[whole(), whole(), whole()],
         out_specs=whole(),
-        out_shape=jax.ShapeDtypeStruct((height, width), jnp.bfloat16),
-        scratch_shapes=[pltpu.VMEM((height * planes, width), jnp.float32)],
+        out_shape=jax.ShapeDtypeStruct((freqs, rows, width), jnp.bfloat16),
+        scratch_shapes=[pltpu.VMEM((rows * planes, width), jnp.float32)] * freqs,
         compiler_params=room(12),
         name="update",
     )(basis, coefficient, model)
 
 
-def sparsify_kernel(mute, cutoff, ahead, back, *rest):
-    spread, (out, planes, returned, wide, narrow) = rest[:-5], rest[-5:]
+def sparsify_body(first_pair, mute, cutoff, ahead, back, arrays, out, planes, returned, wide, narrow):
+    kept, rows, width = arrays[0].shape
+    spread = [array.at[f] for array in arrays for f in range(kept)]
     freq_count = len(spread)
-    rows, width = spread[0].shape
     half = rows // 2
-    kept = out.shape[0]
     terms, sums = 2 * freq_count, returned.shape[0] // half
     is_real = lane_is_real((half, width))
     for k in range(freq_count):
@@ -203,7 +210,7 @@
         wide[...] = jnp.dot(
             ahead[...], values.astype(jnp.bfloat16), preferred_element_type=jnp.float32
         )
-        starts = mute[pl.ds(first, group), :]
+        starts = mute[pl.ds(pl.multiple_of(first_pair + first, group), group), :]
         for r in range(group):
             lanes = pl.ds(r * width, width)
             early = wide[: NT // 2, lanes]
@@ -227,22 +234,56 @@
         out[k, half:] = jnp.where(is_real, pltpu.roll(real_part, width // 2, 1), imag_part)
 
 
-def sparsify(spread, mute, cutoff, ahead, back, kept):
-    rows, width = spread[0].shape
-    terms, sums = 2 * len(spread), back.shape[0]
+def sparsify_kernel(first_pair, mute, cutoff, ahead, back, *rest):
+    sparsify_body(first_pair, mute, cutoff, ahead, back, rest[:-5], *rest[-5:])
+
+
+def sparsify_into_kernel(first_pair, has_before, mute, cutoff, ahead, back, *rest):
+    arrays, out, (piece, stored), scratch = rest[:-7], rest[-7], rest[-6:-4], rest[-4:]
+    if has_before:
+        arrays = arrays[:-1]
+    sparsify_body(first_pair, mute, cutoff, ahead, back, arrays, piece, *scratch)
+    rows = piece.shape[1]
+    copy = pltpu.make_async_copy(piece, out.at[:, pl.ds(2 * first_pair, rows)], stored)
+    copy.start()
+    copy.wait()
+
+
+def sparsify(arrays, mute, cutoff, ahead, back, piece, height=None, before=None):
+    kept, rows, width = arrays[0].shape
+    terms, sums = 2 * kept * len(arrays), back.shape[0]
     group = math.gcd(rows // 2, 32)
+    scratch = [
+        pltpu.VMEM((rows // 2 * terms, width), jnp.float32),
+        pltpu.VMEM((rows // 2 * sums, width), jnp.float32),
+        pltpu.VMEM((NT, group * width), jnp.float32),
+        pltpu.VMEM((NT, group * width), jnp.bfloat16),
+    ]
+    operands = [mute, cutoff, ahead, back, *arrays]
+    in_specs = [whole()] * len(operands)
+    first_pair = piece * rows // 2
+    aliases = {}
+    if height is None:
+        kernel = functools.partial(sparsify_kernel, first_pair)
+        out_spec, out_rows = whole(), rows
+    else:
+        kernel = functools.partial(sparsify_into_kernel, first_pair, before is not None)
+        out_spec, out_rows = pl.BlockSpec(memory_space=pl.ANY), height
+        scratch = [pltpu.VMEM((kept, rows, width), jnp.float32), pltpu.SemaphoreType.DMA] + scratch
+        if before is not None:
+            aliases = {len(operands): 0}
+            operands.append(before)
+            in_specs.append(pl.BlockSpec(memory_space=pl.ANY))
     return pl.pallas_call(
-        sparsify_kernel,
-        out_shape=jax.ShapeDtypeStruct((kept, rows, width), jnp.float32),
-        scratch_shapes=[
-            pltpu.VMEM((rows // 2 * terms, width), jnp.float32),
-            pltpu.VMEM((rows // 2 * sums, width), jnp.float32),
-            pltpu.VMEM((NT, group * width), jnp.float32),
-            pltpu.VMEM((NT, group * width), jnp.bfloat16),
-        ],
+        kernel,
+        in_specs=in_specs,
+        out_specs=out_spec,
+        out_shape=jax.ShapeDtypeStruct((kept, out_rows, width), jnp.float32),
+        scratch_shapes=scratch,
+        input_output_aliases=aliases,
         compiler_params=room(16),
         name="sparsify",
-    )(mute, cutoff, ahead, back, *spread)
+    )(*operands)
 
 
 def wave(shape, sample_dim, freq_count, kept):
@@ -256,8 +297,10 @@
 
 def tables_kernel(kept, freq_count, mute_start, thresholds, mute, cutoff, ahead, back):
     starts = mute_start[...].T
-    half = starts.shape[0] // 2
-    mute[...] = jnp.concatenate([starts[:half], starts[half:]], 1)
+    half = starts.shape[0] // PIECES // 2
+    for piece in range(PIECES):
+        both = starts[2 * half * piece : 2 * half * (piece + 1)]
+        mute[half * piece : half * (piece + 1)] = jnp.concatenate([both[:half], both[half:]], 1)
     cutoff[...] = jnp.concatenate([thresholds[...], thresholds[...]], 1)
     ahead[...] = (wave(ahead.shape, 0, freq_count, kept) / math.sqrt(freq_count)).astype(
         ahead.dtype
@@ -311,19 +354,32 @@
     kept = start_model.shape[0]
     freq_count = kept * lax.axis_size("freq")
     mute, cutoff, ahead, back = tables(mute_start, thresholds, kept, freq_count)
-    freqs = range(kept)
-    model = start_model
+    height = start_model.shape[1]
+    rows = height // PIECES
+    model = [start_model]
     for outer_step in range(OUTER):
-        forward = shuffle(partials(right_basis, model, tile_ranks, outer_step == 0))
-        *misfit, outgoing = residual(
-            left_basis, forward, recorded, tile_ranks, outer_step == OUTER - 1
-        )
+        first, last = outer_step == 0, outer_step == OUTER - 1
+        forward = shuffle(partials(right_basis, model, tile_ranks, first))
+        *misfit, outgoing = residual(left_basis, forward, recorded, tile_ranks, last)
         adjoint = shuffle(outgoing)
-        own = [update(right_basis, adjoint, model, f) for f in freqs]
-        others = [from_others(value) for value in own]
-        spread = own + [others[f][d] for d in range(len(others[0])) for f in freqs]
-        model = sparsify(spread, mute, cutoff, ahead, back, kept)
-    return (model, misfit[0])
+        spread = []
+        for piece in range(PIECES):
+            row = piece * rows
+            before, before_row = (model[0], row) if first else (model[piece], 0)
+            own = update(right_basis, adjoint, before, row, rows, before_row)
+            spread.append([own] + from_others(own))
+        if last:
+            estimate = None
+            for piece in range(PIECES):
+                estimate = sparsify(
+                    spread[piece], mute, cutoff, ahead, back, piece, height, estimate
+                )
+        else:
+            model = [
+                sparsify(spread[piece], mute, cutoff, ahead, back, piece)
+                for piece in range(PIECES)
+            ]
+    return (estimate, misfit[0])
 
 
 def solution(mesh):

time: 161 us -> 157 us (0.975)
  waiting for transfers between devices: 11 us -> 5.64 us
    ppermute x4, waiting for transfers between devices: 11 us -> 5.64 us  [from_others(): lax.ppermute(value, 'freq', [((d + shift) % size, d) for d in range(size)])]
    pallas_call x6 -> x8, Pallas kernels: 26.2 us -> 26.8 us  [the longest x4 22.3 us: sparsify(): pl.pallas_call(kernel, in_specs=in_specs, out_specs=out_spec, out_shape=j...]
  transfers between devices with their start and end apart: 4 -> 4, of which waited for: 4 -> 2; matrix products, arithmetic and copies ran while one was open for 0% -> 0% of each run, Pallas kernels for 2% -> 9%
where the time goes in v3:
time: 157 us
  blocking collectives  99.2 us (63%)
  Pallas kernels  43.8 us (28%)
  waiting for transfers between devices  5.64 us (4%)
  starting transfers between devices  4.31 us (3%)
  local copies, waits for them, and re-layouts  2.83 us (2%)
    all_to_all x4, blocking collectives, shuffle(): lax.all_to_all(partial_value, 'tile', split_axis=0, concat_axis=0, tiled=...  99.2 us
    pallas_call x4, Pallas kernels, sparsify(): pl.pallas_call(kernel, in_specs=in_specs, out_specs=out_spec, out_shape=j...  22.3 us
    pallas_call x2, Pallas kernels, residual(): pl.pallas_call(residual_kernel, in_specs=[pl.BlockSpec(memory_space=pltpu...  9.22 us
    pallas_call x2, Pallas kernels, partials(): pl.pallas_call(first_partials_kernel if first else partials_kernel, in_sp...  7.21 us
    ppermute x4, waiting for transfers between devices, from_others(): lax.ppermute(value, 'freq', [((d + shift) % size, d) for d in range(size)])  5.64 us
    pallas_call x4, Pallas kernels, update(): pl.pallas_call(functools.partial(update_kernel, first_row, model_row), in...  4.51 us
    ppermute x4, starting transfers between devices, from_others(): lax.ppermute(value, 'freq', [((d + shift) % size, d) for d in range(size)])  4.31 us
  transfers between devices with their start and end apart: 4, of which 2 were waited for; matrix products, arithmetic and copies ran while one was open for 0% of the time, Pallas kernels for 9%

profile of v3, /device:TPU:0, one launch (start us, length us, event | category | flops | bytes accessed | tf_op | source)
XLA Modules:
  0.0 156.8 jit_solution(12483352085331026756)
XLA Ops:
  0.6 0.0 copy-start.3
  0.6 0.0 copy-start.2
  0.6 4.9 %partials.2 = bf16[16,2,96,128]{3,2,1,0:T(8,128)(2,1)} custom-call(s32[16,16]{1,0:T(8,128)} %ranks.5, bf16[2,512,2,1536]{3,2,1,0:T(2,128)(2,1)} %basis.13, f32[2,512,128]{2,1,0:T(8,128)} %model.3), custom_call_target="tpu_custom_call" | custom-call | tf_op jit(solution)/shard_map/partials/pallas_call | solution.py:120
  5.6 0.0 slice-start
  5.6 27.8 %all_to_all.20.coefficient = bf16[16,2,96,128]{3,2,1,0:T(8,128)(2,1)S(1)} all-to-all(bf16[16,2,96,128]{3,2,1,0:T(8,128)(2,1)} %partials.2), channel_id=1, replica_groups=mesh['freq'=2,'tile'=16] {'tile'}, dimensions={0} | all-to-all | bytes 1572864 | tf_op jit(solution)/shard_map/all_to_all | solution.py:335
  33.4 2.8 %copy-done = bf16[2,512,2,1536]{3,2,1,0:T(2,128)(2,1)S(1)} copy-done((bf16[2,512,2,1536]{3,2,1,0:T(2,128)(2,1)S(1)}, bf16[2,512,2,1536]{3,2,1,0:T(2,128)(2,1)}, u32[]{:S(2)}) %copy-start) | copy-done | bytes 6291480
  36.2 4.3 %residual.2 = bf16[16,2,96,128]{3,2,1,0:T(8,128)(2,1)S(1)} custom-call(s32[16,16]{1,0:T(8,128)S(1)} %copy-done.3, bf16[2,512,2,1536]{3,2,1,0:T(2,128)(2,1)S(1)} %copy-done, bf16[16,2,96,128]{3,2,1,0:T(8,128)(2,1)S(1)} %all_to_all.20.coefficient, f32[2,512,128]{2,1,0:T(8,128)S(1)} %copy-done.2), custom_call_target="tpu_custom_call" | custom-call | tf_op jit(solution)/shard_map/residual/pallas_call | solution.py:152
  40.5 23.9 %all_to_all.21.coefficient = bf16[16,2,96,128]{3,2,1,0:T(8,128)(2,1)S(1)} all-to-all(bf16[16,2,96,128]{3,2,1,0:T(8,128)(2,1)S(1)} %residual.2), channel_id=1, replica_groups=mesh['freq'=2,'tile'=16] {'tile'}, dimensions={0} | all-to-all | bytes 1572864 | tf_op jit(solution)/shard_map/all_to_all | solution.py:335
  64.3 0.0 copy-start.4
  64.3 0.0 copy-start.5
  64.4 1.1 update.4.rest_0_
  65.5 1.6 collective-permute-start
  67.1 1.1 update.5.rest_0_
  68.2 0.6 collective-permute-start.1
  68.8 0.6 tables.1
  69.5 2.5 %collective-permute-done.rest_1_ = bf16[2,256,128]{2,1,0:T(8,128)(2,1)S(1)} collective-permute-done((bf16[2,256,128]{2,1,0:T(8,128)(2,1)S(1)}, bf16[2,256,128]{2,1,0:T(8,128)(2,1)S(1)}, u32[]{:S(2)}, u32[]{:S(2)}) %collective-permute-start) | collective-permute-done | bytes 131104 | tf_op jit(solution)/shard_map/ppermute | solution.py:348
  71.9 5.2 %sparsify.4.rest_0_.model = f32[2,256,128]{2,1,0:T(8,128)S(1)} custom-call(s32[256,128]{1,0:T(8,128)S(1)} %get-tuple-element.8.mute, f32[1,128]{1,0:T(1,128)S(1)} %get-tuple-element.9.cutoff, bf16[256,8]{1,0:T(8,128)(2,1)S(1)} %get-tuple-element.10.ahead, bf16[8,256]{1,0:T(8,128)(2,1)S(1)} %get-tuple-element.11.back, ...), custom_call_target="tpu_custom_call" | custom-call | tf_op jit(solution)/shard_map/sparsify/pallas_call | solution.py:277
  77.2 0.0 slice-start.3
  77.2 0.0 collective-permute-done.1.rest_1_
  77.2 5.2 %sparsify.5.rest_1_.model = f32[2,256,128]{2,1,0:T(8,128)S(1)} custom-call(s32[256,128]{1,0:T(8,128)S(1)} %get-tuple-element.8.mute, f32[1,128]{1,0:T(1,128)S(1)} %get-tuple-element.9.cutoff, bf16[256,8]{1,0:T(8,128)(2,1)S(1)} %get-tuple-element.10.ahead, bf16[8,256]{1,0:T(8,128)(2,1)S(1)} %get-tuple-element.11.back, ...), custom_call_target="tpu_custom_call" | custom-call | tf_op jit(solution)/shard_map/sparsify/pallas_call | solution.py:277
  82.4 2.3 %partials.3 = bf16[16,2,96,128]{3,2,1,0:T(8,128)(2,1)S(1)} custom-call(s32[16,16]{1,0:T(8,128)S(1)} %copy-done.3, bf16[2,512,2,1536]{3,2,1,0:T(2,128)(2,1)S(1)} %bitcast.3, f32[2,256,128]{2,1,0:T(8,128)S(1)} %sparsify.4.rest_0_.model, f32[2,256,128]{2,1,0:T(8,128)S(1)} %sparsify.5.rest_1_.model), custom_call_target="tpu_custom_call" | custom-call | tf_op jit(solution)/shard_map/partials/pallas_call | solution.py:120
  84.7 23.7 %all_to_all.22.coefficient = bf16[16,2,96,128]{3,2,1,0:T(8,128)(2,1)S(1)} all-to-all(bf16[16,2,96,128]{3,2,1,0:T(8,128)(2,1)S(1)} %partials.3), channel_id=1, replica_groups=mesh['freq'=2,'tile'=16] {'tile'}, dimensions={0} | all-to-all | bytes 1572864 | tf_op jit(solution)/shard_map/all_to_all | solution.py:335
  108.4 4.9 %residual.3 = (f32[2,512,128]{2,1,0:T(8,128)}, bf16[16,2,96,128]{3,2,1,0:T(8,128)(2,1)S(1)}) custom-call(s32[16,16]{1,0:T(8,128)S(1)} %copy-done.3, bf16[2,512,2,1536]{3,2,1,0:T(2,128)(2,1)S(1)} %bitcast.5, bf16[16,2,96,128]{3,2,1,0:T(8,128)(2,1)S(1)} %all_to_all.22.coefficient, f32[2,512,128]{2,1,0:T(8,128)S(1)} %copy-done.2), custom_call_target="tpu_custom_call" | custom-call | tf_op jit(solution)/shard_map/residual/pallas_call | solution.py:152
  113.3 23.8 %all_to_all.23.coefficient = bf16[16,2,96,128]{3,2,1,0:T(8,128)(2,1)S(1)} all-to-all(bf16[16,2,96,128]{3,2,1,0:T(8,128)(2,1)S(1)} %get-tuple-element.12), channel_id=1, replica_groups=mesh['freq'=2,'tile'=16] {'tile'}, dimensions={0} | all-to-all | bytes 1572864 | tf_op jit(solution)/shard_map/all_to_all | solution.py:335
  137.2 1.1 update.7.rest_0_
  138.3 1.7 %collective-permute-start.3 = (bf16[2,256,128]{2,1,0:T(8,128)(2,1)S(1)}, bf16[2,256,128]{2,1,0:T(8,128)(2,1)S(1)}, u32[]{:S(2)}, u32[]{:S(2)}) collective-permute-start(bf16[2,256,128]{2,1,0:T(8,128)(2,1)S(1)} %update.7.rest_0_), channel_id=1, source_target_pairs={{16,0},{0,16},{17,1},{1,17},{18,2},{2,18},{19,3},{3,19},{20,4},{4,... | collective-permute-start | bytes 393224 | tf_op jit(solution)/shard_map/ppermute | solution.py:348
  140.0 1.1 update.6.rest_0_
  141.2 0.4 collective-permute-start.2
  141.6 3.2 %collective-permute-done.3.rest_1_ = bf16[2,256,128]{2,1,0:T(8,128)(2,1)S(1)} collective-permute-done((bf16[2,256,128]{2,1,0:T(8,128)(2,1)S(1)}, bf16[2,256,128]{2,1,0:T(8,128)(2,1)S(1)}, u32[]{:S(2)}, u32[]{:S(2)}) %collective-permute-start.3) | collective-permute-done | bytes 131104 | tf_op jit(solution)/shard_map/ppermute | solution.py:348
  144.7 5.9 %sparsify.6.rest_2_ = f32[2,512,128]{2,1,0:T(8,128)} custom-call(s32[256,128]{1,0:T(8,128)S(1)} %get-tuple-element.8.mute, f32[1,128]{1,0:T(1,128)S(1)} %get-tuple-element.9.cutoff, bf16[256,8]{1,0:T(8,128)(2,1)S(1)} %get-tuple-element.10.ahead, bf16[8,256]{1,0:T(8,128)(2,1)S(1)} %get-tuple-element.11.back, bf16[2,256,128]{2,1,0:T(8,128)(2,1)S(1)} %update.7.rest_0_, ...), custom_call_target="tpu_custom_call" | custom-call | tf_op jit(solution)/shard_map/sparsify/pallas_call | solution.py:277
  150.7 0.0 collective-permute-done.2.rest_1_
  150.7 5.9 %sparsify.7 = f32[2,512,128]{2,1,0:T(8,128)} custom-call(s32[256,128]{1,0:T(8,128)S(1)} %get-tuple-element.8.mute, f32[1,128]{1,0:T(1,128)S(1)} %get-tuple-element.9.cutoff, bf16[256,8]{1,0:T(8,128)(2,1)S(1)} %get-tuple-element.10.ahead, bf16[8,256]{1,0:T(8,128)(2,1)S(1)} %get-tuple-element.11.back, ...), custom_call_target="tpu_custom_call", output_to_operand_aliasing={{}: (6, {})} | custom-call | tf_op jit(solution)/shard_map/sparsify/pallas_call | solution.py:277
  (15 shorter events, 0.0 us)
Async XLA Ops:
  0.6 32.8 %copy-start.3 = (s32[16,16]{1,0:T(8,128)S(1)}, s32[16,16]{1,0:T(8,128)}, u32[]{:S(2)}) copy-start(s32[16,16]{1,0:T(8,128)} %ranks.5) | copy-start | bytes 3076
  0.6 32.8 %copy-start.2 = (f32[2,512,128]{2,1,0:T(8,128)S(1)}, f32[2,512,128]{2,1,0:T(8,128)}, u32[]{:S(2)}) copy-start(f32[2,512,128]{2,1,0:T(8,128)} %recorded.3) | copy-start | bytes 1572868
  5.6 58.8 %slice-start = ((s8[6291456]{0:T(1024)(128)(4,1)}), s8[4194304]{0:T(1024)(128)(4,1)S(1)}, s32[]{:S(2)}) async-start(s8[6291456]{0:T(1024)(128)(4,1)} %bitcast.2), calls=%async_computation.4 | async-start | bytes 8388608
  33.4 2.8 %copy-start = (bf16[2,512,2,1536]{3,2,1,0:T(2,128)(2,1)S(1)}, bf16[2,512,2,1536]{3,2,1,0:T(2,128)(2,1)}, u32[]{:S(2)}) copy-start(bf16[2,512,2,1536]{3,2,1,0:T(2,128)(2,1)} %basis.11) | copy-start | bytes 18874372
  36.2 28.1 %slice-start.1 = ((s8[6291456]{0:T(1024)(128)(4,1)}), s8[2097152]{0:T(1024)(128)(4,1)S(1)}, s32[]{:S(2)}) async-start(s8[6291456]{0:T(1024)(128)(4,1)} %bitcast.2), calls=%async_computation.5 | async-start | bytes 4194304
  36.2 28.1 %copy-start.1 = (f32[2,512,128]{2,1,0:T(8,128)S(1)}, f32[2,512,128]{2,1,0:T(8,128)}, u32[]{:S(2)}) copy-start(f32[2,512,128]{2,1,0:T(8,128)} %model.3) | copy-start | bytes 1572868
  64.3 4.5 %copy-start.4 = (s32[512,64]{0,1:T(8,128)S(1)}, s32[512,64]{0,1:T(8,128)}, u32[]{:S(2)}) copy-start(s32[512,64]{0,1:T(8,128)} %param.12) | copy-start | bytes 393220
  64.3 4.5 %copy-start.5 = (f32[64]{0:T(128)S(1)}, f32[64]{0:T(128)}, u32[]{:S(2)}) copy-start(f32[64]{0:T(128)} %param.13) | copy-start | bytes 772
  65.5 6.4 %collective-permute-start = (bf16[2,256,128]{2,1,0:T(8,128)(2,1)S(1)}, bf16[2,256,128]{2,1,0:T(8,128)(2,1)S(1)}, u32[]{:S(2)}, u32[]{:S(2)}) collective-permute-start(bf16[2,256,128]{2,1,0:T(8,128)(2,1)S(1)} %update.4.rest_0_), channel_id=1, source_target_pairs={{16,0},{0,16},{17,1},{1,17},{18,2},{2,18},{19,3},{3,19},{20,4},{4,... | collective-permute-start | bytes 393224 | tf_op jit(solution)/shard_map/ppermute | solution.py:348
  67.1 41.3 %slice-start.2 = ((s8[6291456]{0:T(1024)(128)(4,1)}), s8[4194304]{0:T(1024)(128)(4,1)S(1)}, s32[]{:S(2)}) async-start(s8[6291456]{0:T(1024)(128)(4,1)} %bitcast.4), calls=%async_computation.6 | async-start | bytes 8388608
  68.2 9.0 %collective-permute-start.1 = (bf16[2,256,128]{2,1,0:T(8,128)(2,1)S(1)}, bf16[2,256,128]{2,1,0:T(8,128)(2,1)S(1)}, u32[]{:S(2)}, u32[]{:S(2)}) collective-permute-start(bf16[2,256,128]{2,1,0:T(8,128)(2,1)S(1)} %update.5.rest_0_), channel_id=1, source_target_pairs={{16,0},{0,16},{17,1},{1,17},{18,2},{2,18},{19,3},{3,19},{20,4},{4,... | collective-permute-start | bytes 393224 | tf_op jit(solution)/shard_map/ppermute | solution.py:348
  77.2 31.2 %slice-start.3 = ((s8[6291456]{0:T(1024)(128)(4,1)}), s8[2097152]{0:T(1024)(128)(4,1)S(1)}, s32[]{:S(2)}) async-start(s8[6291456]{0:T(1024)(128)(4,1)} %bitcast.4), calls=%async_computation.7 | async-start | bytes 4194304
  138.3 6.4 %collective-permute-start.3 = (bf16[2,256,128]{2,1,0:T(8,128)(2,1)S(1)}, bf16[2,256,128]{2,1,0:T(8,128)(2,1)S(1)}, u32[]{:S(2)}, u32[]{:S(2)}) collective-permute-start(bf16[2,256,128]{2,1,0:T(8,128)(2,1)S(1)} %update.7.rest_0_), channel_id=1, source_target_pairs={{16,0},{0,16},{17,1},{1,17},{18,2},{2,18},{19,3},{3,19},{20,4},{4,... | collective-permute-start | bytes 393224 | tf_op jit(solution)/shard_map/ppermute | solution.py:348
  141.2 9.5 %collective-permute-start.2 = (bf16[2,256,128]{2,1,0:T(8,128)(2,1)S(1)}, bf16[2,256,128]{2,1,0:T(8,128)(2,1)S(1)}, u32[]{:S(2)}, u32[]{:S(2)}) collective-permute-start(bf16[2,256,128]{2,1,0:T(8,128)(2,1)S(1)} %update.6.rest_0_), channel_id=1, source_target_pairs={{16,0},{0,16},{17,1},{1,17},{18,2},{2,18},{19,3},{3,19},{20,4},{4,... | collective-permute-start | bytes 393224 | tf_op jit(solution)/shard_map/ppermute | solution.py:348

commit v4 on v3

--- a/solution.py
+++ b/solution.py
@@ -8,10 +8,15 @@
 from jax.experimental.pallas import tpu as pltpu
 from jax.sharding import PartitionSpec as P
 
+
 NT = 256
 OUTER = 2
 STEP_SIZE = 0.5
-PIECES = 2
+
+
+def pieces_of(height):
+    quarter = height // 4
+    return [(0, quarter), (quarter, quarter), (2 * quarter, height - 2 * quarter)]
 
 
 def lane_is_real(shape):
@@ -128,40 +133,62 @@
     )(ranks, basis, *pieces)
 
 
-def residual_kernel(ranks, basis, coefficient, recorded, *rest):
+def residual_kernel(ranks, basis, coefficient, recorded, out, *scratch):
     freqs = basis.shape[0]
-    misfit, out, scratch = rest[: -1 - 2 * freqs], rest[-1 - 2 * freqs], rest[-2 * freqs :]
     block = block_of(ranks.shape[0])
-    values = []
-    for f in range(freqs):
-        values.append(expand(basis[f], coefficient[:, f], scratch[f]) - recorded[f])
-        if misfit:
-            misfit[0][f] = values[f]
+    values = [
+        expand(basis[f], coefficient[:, f], scratch[f]) - recorded[f] for f in range(freqs)
+    ]
     for f in range(freqs):
         contract(
             basis[f], values[f], scratch[freqs + f], lambda tile: ranks[block, tile], out.at[:, f]
         )
 
 
+def last_residual_kernel(ranks, basis, coefficient, recorded, misfit, out, held, stored, *scratch):
+    freqs = basis.shape[0]
+    block = block_of(ranks.shape[0])
+    copies = [
+        pltpu.make_async_copy(held.at[f], misfit.at[f], stored.at[f]) for f in range(freqs)
+    ]
+    for f in range(freqs):
+        held[f] = expand(basis[f], coefficient[:, f], scratch[f]) - recorded[f]
+        copies[f].start()
+    for f in range(freqs):
+        contract(
+            basis[f], held[f], scratch[freqs + f], lambda tile: ranks[block, tile], out.at[:, f]
+        )
+    for copy in copies:
+        copy.wait()
+
+
 def residual(basis, coefficient, recorded, ranks, last):
     freqs, height, planes, _ = basis.shape
-    scratch = pltpu.VMEM((height * planes, recorded.shape[2]), jnp.float32)
+    scratch = [pltpu.VMEM((height * planes, recorded.shape[2]), jnp.float32)] * (2 * freqs)
+    out_specs = [whole()]
     out_shape = [jax.ShapeDtypeStruct(coefficient.shape, jnp.bfloat16)]
     if last:
+        out_specs.insert(0, pl.BlockSpec(memory_space=pl.ANY))
         out_shape.insert(0, jax.ShapeDtypeStruct(recorded.shape, jnp.float32))
+        scratch = [
+            pltpu.VMEM(recorded.shape, jnp.float32),
+            pltpu.SemaphoreType.DMA((freqs,)),
+        ] + scratch
     return pl.pallas_call(
-        residual_kernel,
+        last_residual_kernel if last else residual_kernel,
         in_specs=[pl.BlockSpec(memory_space=pltpu.SMEM), whole(), whole(), whole()],
-        out_specs=[whole()] * len(out_shape),
+        out_specs=out_specs,
         out_shape=out_shape,
-        scratch_shapes=[scratch] * (2 * freqs),
+        scratch_shapes=scratch,
         compiler_params=room(12),
         name="residual",
     )(ranks, basis, coefficient, recorded)
 
 
-def update_kernel(first_row, model_row, basis, coefficient, model, out, *scratch):
-    freqs, rows, _ = out.shape
+def update_kernel(first_row, model_row, basis, coefficient, model, *rest):
+    freqs = basis.shape[0]
+    out, scratch = rest[-1 - freqs], rest[-freqs:]
+    rows = out.shape[1]
     for f in range(freqs):
         part = basis[f, first_row : first_row + rows]
         gradient = expand(part, coefficient[:, f], scratch[f])
@@ -183,7 +210,20 @@
     )(basis, coefficient, model)
 
 
-def sparsify_body(first_pair, mute, cutoff, ahead, back, arrays, out, planes, returned, wide, narrow):
+def sparsify_body(
+    first_pair,
+    mute,
+    cutoff,
+    ahead,
+    back,
+    arrays,
+    out,
+    planes,
+    returned,
+    wide,
+    narrow,
+    finished=lambda f: None,
+):
     kept, rows, width = arrays[0].shape
     spread = [array.at[f] for array in arrays for f in range(kept)]
     freq_count = len(spread)
@@ -232,24 +272,35 @@
         imag_part = returned[pl.ds(2 * k + 1, half, stride=sums), :]
         out[k, :half] = jnp.where(is_real, real_part, pltpu.roll(imag_part, width // 2, 1))
         out[k, half:] = jnp.where(is_real, pltpu.roll(real_part, width // 2, 1), imag_part)
+        finished(k)
 
 
 def sparsify_kernel(first_pair, mute, cutoff, ahead, back, *rest):
     sparsify_body(first_pair, mute, cutoff, ahead, back, rest[:-5], *rest[-5:])
 
 
-def sparsify_into_kernel(first_pair, has_before, mute, cutoff, ahead, back, *rest):
-    arrays, out, (piece, stored), scratch = rest[:-7], rest[-7], rest[-6:-4], rest[-4:]
-    if has_before:
-        arrays = arrays[:-1]
-    sparsify_body(first_pair, mute, cutoff, ahead, back, arrays, piece, *scratch)
-    rows = piece.shape[1]
-    copy = pltpu.make_async_copy(piece, out.at[:, pl.ds(2 * first_pair, rows)], stored)
-    copy.start()
-    copy.wait()
-
-
-def sparsify(arrays, mute, cutoff, ahead, back, piece, height=None, before=None):
+def sparsify_last_kernel(earlier_rows, first_pair, mute, cutoff, ahead, back, *rest):
+    count = len(earlier_rows)
+    arrays, earlier = rest[: -7 - count], rest[-7 - count : -7]
+    out, piece, stored, *scratch = rest[-7:]
+    kept, rows, _ = piece.shape
+    copies = []
+    for place, (row, value) in enumerate(zip(earlier_rows, earlier)):
+        target = out.at[:, pl.ds(row, value.shape[1])]
+        copies.append(pltpu.make_async_copy(value, target, stored.at[kept + place]))
+        copies[-1].start()
+    own = [
+        pltpu.make_async_copy(piece.at[f], out.at[f, pl.ds(2 * first_pair, rows)], stored.at[f])
+        for f in range(kept)
+    ]
+    sparsify_body(
+        first_pair, mute, cutoff, ahead, back, arrays, piece, *scratch, lambda f: own[f].start()
+    )
+    for copy in copies + own:
+        copy.wait()
+
+
+def sparsify(arrays, mute, cutoff, ahead, back, row, height=None, earlier=()):
     kept, rows, width = arrays[0].shape
     terms, sums = 2 * kept * len(arrays), back.shape[0]
     group = math.gcd(rows // 2, 32)
@@ -260,27 +311,23 @@
         pltpu.VMEM((NT, group * width), jnp.bfloat16),
     ]
     operands = [mute, cutoff, ahead, back, *arrays]
-    in_specs = [whole()] * len(operands)
-    first_pair = piece * rows // 2
-    aliases = {}
     if height is None:
-        kernel = functools.partial(sparsify_kernel, first_pair)
+        kernel = functools.partial(sparsify_kernel, row // 2)
         out_spec, out_rows = whole(), rows
     else:
-        kernel = functools.partial(sparsify_into_kernel, first_pair, before is not None)
+        kernel = functools.partial(sparsify_last_kernel, [first for first, _ in earlier], row // 2)
+        operands += [value for _, value in earlier]
         out_spec, out_rows = pl.BlockSpec(memory_space=pl.ANY), height
-        scratch = [pltpu.VMEM((kept, rows, width), jnp.float32), pltpu.SemaphoreType.DMA] + scratch
-        if before is not None:
-            aliases = {len(operands): 0}
-            operands.append(before)
-            in_specs.append(pl.BlockSpec(memory_space=pl.ANY))
+        scratch = [
+            pltpu.VMEM((kept, rows, width), jnp.float32),
+            pltpu.SemaphoreType.DMA((kept + len(earlier),)),
+        ] + scratch
     return pl.pallas_call(
         kernel,
-        in_specs=in_specs,
+        in_specs=[whole()] * len(operands),
         out_specs=out_spec,
         out_shape=jax.ShapeDtypeStruct((kept, out_rows, width), jnp.float32),
         scratch_shapes=scratch,
-        input_output_aliases=aliases,
         compiler_params=room(16),
         name="sparsify",
     )(*operands)
@@ -297,10 +344,9 @@
 
 def tables_kernel(kept, freq_count, mute_start, thresholds, mute, cutoff, ahead, back):
     starts = mute_start[...].T
-    half = starts.shape[0] // PIECES // 2
-    for piece in range(PIECES):
-        both = starts[2 * half * piece : 2 * half * (piece + 1)]
-        mute[half * piece : half * (piece + 1)] = jnp.concatenate([both[:half], both[half:]], 1)
+    for row, rows in pieces_of(starts.shape[0]):
+        upper, lower = starts[row : row + rows // 2], starts[row + rows // 2 : row + rows]
+        mute[row // 2 : (row + rows) // 2] = jnp.concatenate([upper, lower], 1)
     cutoff[...] = jnp.concatenate([thresholds[...], thresholds[...]], 1)
     ahead[...] = (wave(ahead.shape, 0, freq_count, kept) / math.sqrt(freq_count)).astype(
         ahead.dtype
@@ -355,7 +401,7 @@
     freq_count = kept * lax.axis_size("freq")
     mute, cutoff, ahead, back = tables(mute_start, thresholds, kept, freq_count)
     height = start_model.shape[1]
-    rows = height // PIECES
+    pieces = pieces_of(height)
     model = [start_model]
     for outer_step in range(OUTER):
         first, last = outer_step == 0, outer_step == OUTER - 1
@@ -363,23 +409,20 @@
         *misfit, outgoing = residual(left_basis, forward, recorded, tile_ranks, last)
         adjoint = shuffle(outgoing)
         spread = []
-        for piece in range(PIECES):
-            row = piece * rows
+        for piece, (row, rows) in enumerate(pieces):
             before, before_row = (model[0], row) if first else (model[piece], 0)
             own = update(right_basis, adjoint, before, row, rows, before_row)
             spread.append([own] + from_others(own))
-        if last:
-            estimate = None
-            for piece in range(PIECES):
-                estimate = sparsify(
-                    spread[piece], mute, cutoff, ahead, back, piece, height, estimate
-                )
-        else:
-            model = [
-                sparsify(spread[piece], mute, cutoff, ahead, back, piece)
-                for piece in range(PIECES)
-            ]
-    return (estimate, misfit[0])
+        model = []
+        for arrays, (row, rows) in zip(spread, pieces):
+            whole_height, earlier = None, []
+            if last and row + rows == height:
+                whole_height = height
+                earlier = [(first_row, value) for (first_row, _), value in zip(pieces, model)]
+            model.append(
+                sparsify(arrays, mute, cutoff, ahead, back, row, whole_height, earlier)
+            )
+    return (model[-1], misfit[0])
 
 
 def solution(mesh):

time: 157 us -> 160 us (1.019)
  starting transfers between devices: 4.31 us -> 7.42 us
    ppermute x4 -> x6, starting transfers between devices: 4.31 us -> 7.42 us  [from_others(): lax.ppermute(value, 'freq', [((d + shift) % size, d) for d in range(size)])]
    ppermute x4 -> x6, waiting for transfers between devices: 5.64 us -> 4.85 us  [from_others(): lax.ppermute(value, 'freq', [((d + shift) % size, d) for d in range(size)])]
    pallas_call x6 -> x8, Pallas kernels: 31.5 us -> 30.8 us  [the longest x6 21.8 us: sparsify(): pl.pallas_call(kernel, in_specs=[whole()] * len(operands), out_specs=out_...]
    pallas_call x4 -> x6, Pallas kernels: 4.51 us -> 5.02 us  [update(): pl.pallas_call(functools.partial(update_kernel, first_row, model_row), in...]
  transfers between devices with their start and end apart: 4 -> 6, of which waited for: 2 -> 2; matrix products, arithmetic and copies ran while one was open for 0% -> 0% of each run, Pallas kernels for 9% -> 9%
where the time goes in v4:
time: 160 us; the launch traced here: 159 us
  blocking collectives  99.4 us (62%)
  Pallas kernels  43.7 us (27%)
  starting transfers between devices  7.42 us (5%)
  waiting for transfers between devices  4.85 us (3%)
  local copies, waits for them, and re-layouts  2.83 us (2%)
    all_to_all x4, blocking collectives, shuffle(): lax.all_to_all(partial_value, 'tile', split_axis=0, concat_axis=0, tiled=...  99.4 us
    pallas_call x6, Pallas kernels, sparsify(): pl.pallas_call(kernel, in_specs=[whole()] * len(operands), out_specs=out_...  21.8 us
    pallas_call x2, Pallas kernels, residual(): pl.pallas_call(last_residual_kernel if last else residual_kernel, in_spec...  9.08 us
    ppermute x6, starting transfers between devices, from_others(): lax.ppermute(value, 'freq', [((d + shift) % size, d) for d in range(size)])  7.42 us
    pallas_call x2, Pallas kernels, partials(): pl.pallas_call(first_partials_kernel if first else partials_kernel, in_sp...  7.2 us
    pallas_call x6, Pallas kernels, update(): pl.pallas_call(functools.partial(update_kernel, first_row, model_row), in...  5.02 us
    ppermute x6, waiting for transfers between devices, from_others(): lax.ppermute(value, 'freq', [((d + shift) % size, d) for d in range(size)])  4.85 us
  transfers between devices with their start and end apart: 6, of which 2 were waited for; matrix products, arithmetic and copies ran while one was open for 0% of the time, Pallas kernels for 9%

profile of v4, /device:TPU:0, one launch (start us, length us, event | category | flops | bytes accessed | tf_op | source)
XLA Modules:
  0.0 159.2 jit_solution(13218146653553106869)
XLA Ops:
  0.6 4.9 %partials.2 = bf16[16,2,96,128]{3,2,1,0:T(8,128)(2,1)} custom-call(s32[16,16]{1,0:T(8,128)} %ranks.5, bf16[2,512,2,1536]{3,2,1,0:T(2,128)(2,1)} %basis.17, f32[2,512,128]{2,1,0:T(8,128)} %model.5), custom_call_target="tpu_custom_call" | custom-call | tf_op jit(solution)/shard_map/partials/pallas_call | solution.py:125
  5.6 0.0 slice-start
  5.6 27.8 %all_to_all.20.coefficient = bf16[16,2,96,128]{3,2,1,0:T(8,128)(2,1)S(1)} all-to-all(bf16[16,2,96,128]{3,2,1,0:T(8,128)(2,1)} %partials.2), channel_id=1, replica_groups=mesh['freq'=2,'tile'=16] {'tile'}, dimensions={0} | all-to-all | bytes 1572864 | tf_op jit(solution)/shard_map/all_to_all | solution.py:381
  33.4 2.8 %copy-done = bf16[2,512,2,1536]{3,2,1,0:T(2,128)(2,1)S(1)} copy-done((bf16[2,512,2,1536]{3,2,1,0:T(2,128)(2,1)S(1)}, bf16[2,512,2,1536]{3,2,1,0:T(2,128)(2,1)}, u32[]{:S(2)}) %copy-start) | copy-done | bytes 6291480
  36.2 4.3 %residual.2 = bf16[16,2,96,128]{3,2,1,0:T(8,128)(2,1)S(1)} custom-call(s32[16,16]{1,0:T(8,128)S(1)} %copy-done.3, bf16[2,512,2,1536]{3,2,1,0:T(2,128)(2,1)S(1)} %copy-done, bf16[16,2,96,128]{3,2,1,0:T(8,128)(2,1)S(1)} %all_to_all.20.coefficient, f32[2,512,128]{2,1,0:T(8,128)S(1)} %copy-done.2), custom_call_target="tpu_custom_call" | custom-call | tf_op jit(solution)/shard_map/residual/pallas_call | solution.py:177
  40.4 23.9 %all_to_all.21.coefficient = bf16[16,2,96,128]{3,2,1,0:T(8,128)(2,1)S(1)} all-to-all(bf16[16,2,96,128]{3,2,1,0:T(8,128)(2,1)S(1)} %residual.2), channel_id=1, replica_groups=mesh['freq'=2,'tile'=16] {'tile'}, dimensions={0} | all-to-all | bytes 1572864 | tf_op jit(solution)/shard_map/all_to_all | solution.py:381
  64.3 1.1 update.8.rest_0_
  65.5 1.6 collective-permute-start.2
  67.1 0.7 update.6.rest_0_
  67.7 0.6 collective-permute-start
  68.4 0.7 update.7.rest_0_
  69.0 1.6 collective-permute-start.1
  70.6 0.6 tables.1
  71.3 2.1 %collective-permute-done.rest_1_ = bf16[2,128,128]{2,1,0:T(8,128)(2,1)S(1)} collective-permute-done((bf16[2,128,128]{2,1,0:T(8,128)(2,1)S(1)}, bf16[2,128,128]{2,1,0:T(8,128)(2,1)S(1)}, u32[]{:S(2)}, u32[]{:S(2)}) %collective-permute-start) | collective-permute-done | bytes 65568 | tf_op jit(solution)/shard_map/ppermute | solution.py:394
  73.3 2.7 %sparsify.6.rest_0_.model = f32[2,128,128]{2,1,0:T(8,128)S(1)} custom-call(s32[256,128]{1,0:T(8,128)S(1)} %get-tuple-element.8.mute, f32[1,128]{1,0:T(1,128)S(1)} %get-tuple-element.9.cutoff, bf16[256,8]{1,0:T(8,128)(2,1)S(1)} %get-tuple-element.10.ahead, bf16[8,256]{1,0:T(8,128)(2,1)S(1)} %get-tuple-element.11.back, ...), custom_call_target="tpu_custom_call" | custom-call | tf_op jit(solution)/shard_map/sparsify/pallas_call | solution.py:325
  76.0 2.7 %sparsify.7.rest_1_.model = f32[2,128,128]{2,1,0:T(8,128)S(1)} custom-call(s32[256,128]{1,0:T(8,128)S(1)} %get-tuple-element.8.mute, f32[1,128]{1,0:T(1,128)S(1)} %get-tuple-element.9.cutoff, bf16[256,8]{1,0:T(8,128)(2,1)S(1)} %get-tuple-element.10.ahead, bf16[8,256]{1,0:T(8,128)(2,1)S(1)} %get-tuple-element.11.back, ...), custom_call_target="tpu_custom_call" | custom-call | tf_op jit(solution)/shard_map/sparsify/pallas_call | solution.py:325
  78.7 0.0 slice-start.3
  78.7 5.2 %sparsify.8.rest_2_.model = f32[2,256,128]{2,1,0:T(8,128)S(1)} custom-call(s32[256,128]{1,0:T(8,128)S(1)} %get-tuple-element.8.mute, f32[1,128]{1,0:T(1,128)S(1)} %get-tuple-element.9.cutoff, bf16[256,8]{1,0:T(8,128)(2,1)S(1)} %get-tuple-element.10.ahead, bf16[8,256]{1,0:T(8,128)(2,1)S(1)} %get-tuple-element.11.back, ...), custom_call_target="tpu_custom_call" | custom-call | tf_op jit(solution)/shard_map/sparsify/pallas_call | solution.py:325
  83.9 2.3 %partials.3 = bf16[16,2,96,128]{3,2,1,0:T(8,128)(2,1)S(1)} custom-call(s32[16,16]{1,0:T(8,128)S(1)} %copy-done.3, bf16[2,512,2,1536]{3,2,1,0:T(2,128)(2,1)S(1)} %bitcast.3, f32[2,128,128]{2,1,0:T(8,128)S(1)} %sparsify.6.rest_0_.model, f32[2,128,128]{2,1,0:T(8,128)S(1)} %sparsify.7.rest_1_.model, f32[2,256,128]{2,1,0:T(8,128)S(1)} %sparsify.8.rest_2_.model), custom_call_target="tpu_custom_call" | custom-call | tf_op jit(solution)/shard_map/partials/pallas_call | solution.py:125
  86.2 23.9 %all_to_all.22.coefficient = bf16[16,2,96,128]{3,2,1,0:T(8,128)(2,1)S(1)} all-to-all(bf16[16,2,96,128]{3,2,1,0:T(8,128)(2,1)S(1)} %partials.3), channel_id=1, replica_groups=mesh['freq'=2,'tile'=16] {'tile'}, dimensions={0} | all-to-all | bytes 1572864 | tf_op jit(solution)/shard_map/all_to_all | solution.py:381
  110.1 4.8 %residual.3 = (f32[2,512,128]{2,1,0:T(8,128)}, bf16[16,2,96,128]{3,2,1,0:T(8,128)(2,1)S(1)}) custom-call(s32[16,16]{1,0:T(8,128)S(1)} %copy-done.3, bf16[2,512,2,1536]{3,2,1,0:T(2,128)(2,1)S(1)} %bitcast.5, bf16[16,2,96,128]{3,2,1,0:T(8,128)(2,1)S(1)} %all_to_all.22.coefficient, f32[2,512,128]{2,1,0:T(8,128)S(1)} %copy-done.2), custom_call_target="tpu_custom_call" | custom-call | tf_op jit(solution)/shard_map/residual/pallas_call | solution.py:177
  114.9 23.9 %all_to_all.23.coefficient = bf16[16,2,96,128]{3,2,1,0:T(8,128)(2,1)S(1)} all-to-all(bf16[16,2,96,128]{3,2,1,0:T(8,128)(2,1)S(1)} %get-tuple-element.12), channel_id=1, replica_groups=mesh['freq'=2,'tile'=16] {'tile'}, dimensions={0} | all-to-all | bytes 1572864 | tf_op jit(solution)/shard_map/all_to_all | solution.py:381
  138.8 1.1 update.9.rest_0_
  139.9 1.6 collective-permute-start.3
  141.5 0.7 update.10.rest_0_
  142.1 0.6 collective-permute-start.4
  142.7 0.7 update.11.rest_0_
  143.4 1.6 collective-permute-start.5
  145.0 2.8 %collective-permute-done.4.rest_1_ = bf16[2,128,128]{2,1,0:T(8,128)(2,1)S(1)} collective-permute-done((bf16[2,128,128]{2,1,0:T(8,128)(2,1)S(1)}, bf16[2,128,128]{2,1,0:T(8,128)(2,1)S(1)}, u32[]{:S(2)}, u32[]{:S(2)}) %collective-permute-start.4) | collective-permute-done | bytes 65568 | tf_op jit(solution)/shard_map/ppermute | solution.py:394
  147.7 2.7 %sparsify.9.rest_2_ = f32[2,128,128]{2,1,0:T(8,128)S(1)} custom-call(s32[256,128]{1,0:T(8,128)S(1)} %get-tuple-element.8.mute, f32[1,128]{1,0:T(1,128)S(1)} %get-tuple-element.9.cutoff, bf16[256,8]{1,0:T(8,128)(2,1)S(1)} %get-tuple-element.10.ahead, bf16[8,256]{1,0:T(8,128)(2,1)S(1)} %get-tuple-element.11.back, bf16[2,128,128]{2,1,0:T(8,128)(2,1)S(1)} %update.10.rest_0_, ...), custom_call_target="tpu_custom_call" | custom-call | tf_op jit(solution)/shard_map/sparsify/pallas_call | solution.py:325
  150.4 2.7 %sparsify.10.rest_3_ = f32[2,128,128]{2,1,0:T(8,128)S(1)} custom-call(s32[256,128]{1,0:T(8,128)S(1)} %get-tuple-element.8.mute, f32[1,128]{1,0:T(1,128)S(1)} %get-tuple-element.9.cutoff, bf16[256,8]{1,0:T(8,128)(2,1)S(1)} %get-tuple-element.10.ahead, bf16[8,256]{1,0:T(8,128)(2,1)S(1)} %get-tuple-element.11.back, bf16[2,128,128]{2,1,0:T(8,128)(2,1)S(1)} %update.11.rest_0_, ...), custom_call_target="tpu_custom_call" | custom-call | tf_op jit(solution)/shard_map/sparsify/pallas_call | solution.py:325
  153.1 5.9 %sparsify.11 = f32[2,512,128]{2,1,0:T(8,128)} custom-call(s32[256,128]{1,0:T(8,128)S(1)} %get-tuple-element.8.mute, f32[1,128]{1,0:T(1,128)S(1)} %get-tuple-element.9.cutoff, bf16[256,8]{1,0:T(8,128)(2,1)S(1)} %get-tuple-element.10.ahead, bf16[8,256]{1,0:T(8,128)(2,1)S(1)} %get-tuple-element.11.back, bf16[2,256,128]{2,1,0:T(8,128)(2,1)S(1)} %update.9.rest_0_, ...), custom_call_target="tpu_custom_call" | custom-call | tf_op jit(solution)/shard_map/sparsify/pallas_call | solution.py:325
  (23 shorter events, 0.0 us)
Async XLA Ops:
  0.6 32.8 %copy-start.3 = (s32[16,16]{1,0:T(8,128)S(1)}, s32[16,16]{1,0:T(8,128)}, u32[]{:S(2)}) copy-start(s32[16,16]{1,0:T(8,128)} %ranks.5) | copy-start | bytes 3076
  0.6 32.7 %copy-start.2 = (f32[2,512,128]{2,1,0:T(8,128)S(1)}, f32[2,512,128]{2,1,0:T(8,128)}, u32[]{:S(2)}) copy-start(f32[2,512,128]{2,1,0:T(8,128)} %recorded.3) | copy-start | bytes 1572868
  5.6 58.8 %slice-start = ((s8[6291456]{0:T(1024)(128)(4,1)}), s8[4194304]{0:T(1024)(128)(4,1)S(1)}, s32[]{:S(2)}) async-start(s8[6291456]{0:T(1024)(128)(4,1)} %bitcast.2), calls=%async_computation.4 | async-start | bytes 8388608
  33.4 2.8 %copy-start = (bf16[2,512,2,1536]{3,2,1,0:T(2,128)(2,1)S(1)}, bf16[2,512,2,1536]{3,2,1,0:T(2,128)(2,1)}, u32[]{:S(2)}) copy-start(bf16[2,512,2,1536]{3,2,1,0:T(2,128)(2,1)} %basis.14) | copy-start | bytes 18874372
  36.2 28.1 %slice-start.1 = ((s8[6291456]{0:T(1024)(128)(4,1)}), s8[2097152]{0:T(1024)(128)(4,1)S(1)}, s32[]{:S(2)}) async-start(s8[6291456]{0:T(1024)(128)(4,1)} %bitcast.2), calls=%async_computation.5 | async-start | bytes 4194304
  36.2 28.1 %copy-start.1 = (f32[2,512,128]{2,1,0:T(8,128)S(1)}, f32[2,512,128]{2,1,0:T(8,128)}, u32[]{:S(2)}) copy-start(f32[2,512,128]{2,1,0:T(8,128)} %model.5) | copy-start | bytes 1572868
  65.5 5.1 %copy-start.4 = (s32[512,64]{0,1:T(8,128)S(1)}, s32[512,64]{0,1:T(8,128)}, u32[]{:S(2)}) copy-start(s32[512,64]{0,1:T(8,128)} %param.12) | copy-start | bytes 393220
  65.5 5.1 %copy-start.5 = (f32[64]{0:T(128)S(1)}, f32[64]{0:T(128)}, u32[]{:S(2)}) copy-start(f32[64]{0:T(128)} %param.13) | copy-start | bytes 772
  65.5 13.2 %collective-permute-start.2 = (bf16[2,256,128]{2,1,0:T(8,128)(2,1)S(1)}, bf16[2,256,128]{2,1,0:T(8,128)(2,1)S(1)}, u32[]{:S(2)}, u32[]{:S(2)}) collective-permute-start(bf16[2,256,128]{2,1,0:T(8,128)(2,1)S(1)} %update.8.rest_0_), channel_id=1, source_target_pairs={{16,0},{0,16},{17,1},{1,17},{18,2},{2,18},{19,3},{3,19},{20,4},{4,... | collective-permute-start | bytes 393224 | tf_op jit(solution)/shard_map/ppermute | solution.py:394
  67.7 5.6 %collective-permute-start = (bf16[2,128,128]{2,1,0:T(8,128)(2,1)S(1)}, bf16[2,128,128]{2,1,0:T(8,128)(2,1)S(1)}, u32[]{:S(2)}, u32[]{:S(2)}) collective-permute-start(bf16[2,128,128]{2,1,0:T(8,128)(2,1)S(1)} %update.6.rest_0_), channel_id=1, source_target_pairs={{16,0},{0,16},{17,1},{1,17},{18,2},{2,18},{19,3},{3,19},{20,4},{4,... | collective-permute-start | bytes 196616 | tf_op jit(solution)/shard_map/ppermute | solution.py:394
  68.3 41.8 %slice-start.2 = ((s8[6291456]{0:T(1024)(128)(4,1)}), s8[4194304]{0:T(1024)(128)(4,1)S(1)}, s32[]{:S(2)}) async-start(s8[6291456]{0:T(1024)(128)(4,1)} %bitcast.4), calls=%async_computation.6 | async-start | bytes 8388608
  69.0 7.0 %collective-permute-start.1 = (bf16[2,128,128]{2,1,0:T(8,128)(2,1)S(1)}, bf16[2,128,128]{2,1,0:T(8,128)(2,1)S(1)}, u32[]{:S(2)}, u32[]{:S(2)}) collective-permute-start(bf16[2,128,128]{2,1,0:T(8,128)(2,1)S(1)} %update.7.rest_0_), channel_id=1, source_target_pairs={{16,0},{0,16},{17,1},{1,17},{18,2},{2,18},{19,3},{3,19},{20,4},{4,... | collective-permute-start | bytes 196616 | tf_op jit(solution)/shard_map/ppermute | solution.py:394
  78.7 31.4 %slice-start.3 = ((s8[6291456]{0:T(1024)(128)(4,1)}), s8[2097152]{0:T(1024)(128)(4,1)S(1)}, s32[]{:S(2)}) async-start(s8[6291456]{0:T(1024)(128)(4,1)} %bitcast.4), calls=%async_computation.7 | async-start | bytes 4194304
  139.9 13.2 %collective-permute-start.3 = (bf16[2,256,128]{2,1,0:T(8,128)(2,1)S(1)}, bf16[2,256,128]{2,1,0:T(8,128)(2,1)S(1)}, u32[]{:S(2)}, u32[]{:S(2)}) collective-permute-start(bf16[2,256,128]{2,1,0:T(8,128)(2,1)S(1)} %update.9.rest_0_), channel_id=1, source_target_pairs={{16,0},{0,16},{17,1},{1,17},{18,2},{2,18},{19,3},{3,19},{20,4},{4,... | collective-permute-start | bytes 393224 | tf_op jit(solution)/shard_map/ppermute | solution.py:394
  142.1 5.6 %collective-permute-start.4 = (bf16[2,128,128]{2,1,0:T(8,128)(2,1)S(1)}, bf16[2,128,128]{2,1,0:T(8,128)(2,1)S(1)}, u32[]{:S(2)}, u32[]{:S(2)}) collective-permute-start(bf16[2,128,128]{2,1,0:T(8,128)(2,1)S(1)} %update.10.rest_0_), channel_id=1, source_target_pairs={{16,0},{0,16},{17,1},{1,17},{18,2},{2,18},{19,3},{3,19},{20,4},{4,... | collective-permute-start | bytes 196616 | tf_op jit(solution)/shard_map/ppermute | solution.py:394
  143.4 7.0 %collective-permute-start.5 = (bf16[2,128,128]{2,1,0:T(8,128)(2,1)S(1)}, bf16[2,128,128]{2,1,0:T(8,128)(2,1)S(1)}, u32[]{:S(2)}, u32[]{:S(2)}) collective-permute-start(bf16[2,128,128]{2,1,0:T(8,128)(2,1)S(1)} %update.11.rest_0_), channel_id=1, source_target_pairs={{16,0},{0,16},{17,1},{1,17},{18,2},{2,18},{19,3},{3,19},{20,4},{4,... | collective-permute-start | bytes 196616 | tf_op jit(solution)/shard_map/ppermute | solution.py:394

commit v5 on v4

--- a/solution.py
+++ b/solution.py
@@ -128,7 +128,7 @@
         out_specs=whole(),
         out_shape=jax.ShapeDtypeStruct((inside, freqs, columns // inside, width), jnp.bfloat16),
         scratch_shapes=scratch,
-        compiler_params=room(60 if first else 12),
+        compiler_params=room(54 if first else 12),
         name="partials",
     )(ranks, basis, *pieces)
 
@@ -342,7 +342,7 @@
     return jnp.cos(phases * (2.0 * math.pi / NT))
 
 
-def tables_kernel(kept, freq_count, mute_start, thresholds, mute, cutoff, ahead, back):
+def tables_kernel(kept, freq_count, mute_start, thresholds, _, mute, cutoff, ahead, back):
     starts = mute_start[...].T
     for row, rows in pieces_of(starts.shape[0]):
         upper, lower = starts[row : row + rows // 2], starts[row + rows // 2 : row + rows]
@@ -355,12 +355,12 @@
     back[...] = (wave(back.shape, 1, freq_count, kept) * scale).astype(back.dtype)
 
 
-def tables(mute_start, thresholds, kept, freq_count):
+def tables(mute_start, thresholds, after, kept, freq_count):
     height, sources = mute_start.shape
     sums = -(-2 * kept // 8) * 8
     return pl.pallas_call(
         functools.partial(tables_kernel, kept, freq_count),
-        in_specs=[whole(), whole()],
+        in_specs=[whole(), whole(), pl.BlockSpec(memory_space=pl.ANY)],
         out_specs=[whole()] * 4,
         out_shape=[
             jax.ShapeDtypeStruct((height // 2, 2 * sources), jnp.int32),
@@ -369,8 +369,9 @@
             jax.ShapeDtypeStruct((sums, NT), jnp.bfloat16),
         ],
         compiler_params=room(4),
+        cost_estimate=pl.CostEstimate(flops=4 * 10**9, transcendentals=0, bytes_accessed=2**23),
         name="tables",
-    )(mute_start.T, thresholds[None])
+    )(mute_start.T, thresholds[None], after)
 
 
 def shuffle(partial_value):
@@ -399,13 +400,15 @@
 def body(left_basis, right_basis, start_model, recorded, tile_ranks, mute_start, thresholds):
     kept = start_model.shape[0]
     freq_count = kept * lax.axis_size("freq")
-    mute, cutoff, ahead, back = tables(mute_start, thresholds, kept, freq_count)
     height = start_model.shape[1]
     pieces = pieces_of(height)
     model = [start_model]
     for outer_step in range(OUTER):
         first, last = outer_step == 0, outer_step == OUTER - 1
-        forward = shuffle(partials(right_basis, model, tile_ranks, first))
+        outgoing = partials(right_basis, model, tile_ranks, first)
+        if first:
+            mute, cutoff, ahead, back = tables(mute_start, thresholds, outgoing, kept, freq_count)
+        forward = shuffle(outgoing)
         *misfit, outgoing = residual(left_basis, forward, recorded, tile_ranks, last)
         adjoint = shuffle(outgoing)
         spread = []
@@ -419,9 +422,7 @@
             if last and row + rows == height:
                 whole_height = height
                 earlier = [(first_row, value) for (first_row, _), value in zip(pieces, model)]
-            model.append(
-                sparsify(arrays, mute, cutoff, ahead, back, row, whole_height, earlier)
-            )
+            model.append(sparsify(arrays, mute, cutoff, ahead, back, row, whole_height, earlier))
     return (model[-1], misfit[0])
 
 

time: 160 us -> 155 us (0.969)
  local copies, waits for them, and re-layouts: 2.83 us -> 0.05 us
    unnamed x20 -> x18, local copies, waits for them, and re-layouts: 2.83 us -> 0.05 us
where the time goes in v5:
time: 155 us
  blocking collectives  99.3 us (64%)
  Pallas kernels  43.6 us (28%)
  starting transfers between devices  6.37 us (4%)
  waiting for transfers between devices  4.58 us (3%)
    all_to_all x4, blocking collectives, shuffle(): lax.all_to_all(partial_value, 'tile', split_axis=0, concat_axis=0, tiled=...  99.3 us
    pallas_call x6, Pallas kernels, sparsify(): pl.pallas_call(kernel, in_specs=[whole()] * len(operands), out_specs=out_...  21.8 us
    pallas_call x2, Pallas kernels, residual(): pl.pallas_call(last_residual_kernel if last else residual_kernel, in_spec...  8.92 us
    pallas_call x2, Pallas kernels, partials(): pl.pallas_call(first_partials_kernel if first else partials_kernel, in_sp...  7.28 us
    ppermute x6, starting transfers between devices, from_others(): lax.ppermute(value, 'freq', [((d + shift) % size, d) for d in range(size)])  6.37 us
    pallas_call x6, Pallas kernels, update(): pl.pallas_call(functools.partial(update_kernel, first_row, model_row), in...  4.97 us
    ppermute x6, waiting for transfers between devices, from_others(): lax.ppermute(value, 'freq', [((d + shift) % size, d) for d in range(size)])  4.58 us
  transfers between devices with their start and end apart: 6, of which 2 were waited for; matrix products, arithmetic and copies ran while one was open for 0% of the time, Pallas kernels for 9%

profile of v5, /device:TPU:0, one launch (start us, length us, event | category | flops | bytes accessed | tf_op | source)
XLA Modules:
  0.0 155.0 jit_solution(7001281891202478093)
XLA Ops:
  0.7 5.0 %partials.2._ = bf16[16,2,96,128]{3,2,1,0:T(8,128)(2,1)} custom-call(s32[16,16]{1,0:T(8,128)} %ranks.5, bf16[2,512,2,1536]{3,2,1,0:T(2,128)(2,1)} %basis.17, f32[2,512,128]{2,1,0:T(8,128)} %model.5), custom_call_target="tpu_custom_call" | custom-call | tf_op jit(solution)/shard_map/partials/pallas_call | solution.py:125
  5.7 0.0 slice-start
  5.7 27.8 %all_to_all.20.coefficient = bf16[16,2,96,128]{3,2,1,0:T(8,128)(2,1)S(1)} all-to-all(bf16[16,2,96,128]{3,2,1,0:T(8,128)(2,1)} %partials.2._), channel_id=1, replica_groups=mesh['freq'=2,'tile'=16] {'tile'}, dimensions={0} | all-to-all | bytes 1572864 | tf_op jit(solution)/shard_map/all_to_all | solution.py:382
  33.5 0.0 slice-start.1
  33.5 4.2 %residual.2 = bf16[16,2,96,128]{3,2,1,0:T(8,128)(2,1)S(1)} custom-call(s32[16,16]{1,0:T(8,128)S(1)} %copy-done.4, bf16[2,512,2,1536]{3,2,1,0:T(2,128)(2,1)S(1)} %copy-done, bf16[16,2,96,128]{3,2,1,0:T(8,128)(2,1)S(1)} %all_to_all.20.coefficient, f32[2,512,128]{2,1,0:T(8,128)S(1)} %copy-done.3), custom_call_target="tpu_custom_call" | custom-call | tf_op jit(solution)/shard_map/residual/pallas_call | solution.py:177
  37.7 23.9 %all_to_all.21.coefficient = bf16[16,2,96,128]{3,2,1,0:T(8,128)(2,1)S(1)} all-to-all(bf16[16,2,96,128]{3,2,1,0:T(8,128)(2,1)S(1)} %residual.2), channel_id=1, replica_groups=mesh['freq'=2,'tile'=16] {'tile'}, dimensions={0} | all-to-all | bytes 1572864 | tf_op jit(solution)/shard_map/all_to_all | solution.py:382
  61.6 0.7 update.6.rest_0_
  62.3 0.0 copy-start.5
  62.3 1.6 %collective-permute-start = (bf16[2,128,128]{2,1,0:T(8,128)(2,1)S(1)}, bf16[2,128,128]{2,1,0:T(8,128)(2,1)S(1)}, u32[]{:S(2)}, u32[]{:S(2)}) collective-permute-start(bf16[2,128,128]{2,1,0:T(8,128)(2,1)S(1)} %update.6.rest_0_), channel_id=1, source_target_pairs={{16,0},{0,16},{17,1},{1,17},{18,2},{2,18},{19,3},{3,19},{20,4},{4,... | collective-permute-start | bytes 196616 | tf_op jit(solution)/shard_map/ppermute | solution.py:395
  63.9 0.7 update.7.rest_0_
  64.5 0.6 collective-permute-start.1
  65.1 1.1 update.8.rest_0_
  66.3 1.6 %collective-permute-start.2 = (bf16[2,256,128]{2,1,0:T(8,128)(2,1)S(1)}, bf16[2,256,128]{2,1,0:T(8,128)(2,1)S(1)}, u32[]{:S(2)}, u32[]{:S(2)}) collective-permute-start(bf16[2,256,128]{2,1,0:T(8,128)(2,1)S(1)} %update.8.rest_0_), channel_id=1, source_target_pairs={{16,0},{0,16},{17,1},{1,17},{18,2},{2,18},{19,3},{3,19},{20,4},{4,... | collective-permute-start | bytes 393224 | tf_op jit(solution)/shard_map/ppermute | solution.py:395
  67.8 0.6 tables.1
  68.5 0.8 collective-permute-done.1.rest_1_
  69.2 2.7 %sparsify.7.rest_1_.model = f32[2,128,128]{2,1,0:T(8,128)S(1)} custom-call(s32[256,128]{1,0:T(8,128)S(1)} %get-tuple-element.8.mute, f32[1,128]{1,0:T(1,128)S(1)} %get-tuple-element.9.cutoff, bf16[256,8]{1,0:T(8,128)(2,1)S(1)} %get-tuple-element.10.ahead, bf16[8,256]{1,0:T(8,128)(2,1)S(1)} %get-tuple-element.11.back, ...), custom_call_target="tpu_custom_call" | custom-call | tf_op jit(solution)/shard_map/sparsify/pallas_call | solution.py:325
  71.9 2.7 %sparsify.6.rest_0_.model = f32[2,128,128]{2,1,0:T(8,128)S(1)} custom-call(s32[256,128]{1,0:T(8,128)S(1)} %get-tuple-element.8.mute, f32[1,128]{1,0:T(1,128)S(1)} %get-tuple-element.9.cutoff, bf16[256,8]{1,0:T(8,128)(2,1)S(1)} %get-tuple-element.10.ahead, bf16[8,256]{1,0:T(8,128)(2,1)S(1)} %get-tuple-element.11.back, ...), custom_call_target="tpu_custom_call" | custom-call | tf_op jit(solution)/shard_map/sparsify/pallas_call | solution.py:325
  74.6 5.2 %sparsify.8.rest_2_.model = f32[2,256,128]{2,1,0:T(8,128)S(1)} custom-call(s32[256,128]{1,0:T(8,128)S(1)} %get-tuple-element.8.mute, f32[1,128]{1,0:T(1,128)S(1)} %get-tuple-element.9.cutoff, bf16[256,8]{1,0:T(8,128)(2,1)S(1)} %get-tuple-element.10.ahead, bf16[8,256]{1,0:T(8,128)(2,1)S(1)} %get-tuple-element.11.back, ...), custom_call_target="tpu_custom_call" | custom-call | tf_op jit(solution)/shard_map/sparsify/pallas_call | solution.py:325
  79.8 2.3 %partials.3 = bf16[16,2,96,128]{3,2,1,0:T(8,128)(2,1)S(1)} custom-call(s32[16,16]{1,0:T(8,128)S(1)} %copy-done.4, bf16[2,512,2,1536]{3,2,1,0:T(2,128)(2,1)S(1)} %bitcast.3, f32[2,128,128]{2,1,0:T(8,128)S(1)} %sparsify.6.rest_0_.model, f32[2,128,128]{2,1,0:T(8,128)S(1)} %sparsify.7.rest_1_.model, f32[2,256,128]{2,1,0:T(8,128)S(1)} %sparsify.8.rest_2_.model), custom_call_target="tpu_custom_call" | custom-call | tf_op jit(solution)/shard_map/partials/pallas_call | solution.py:125
  82.1 23.8 %all_to_all.22.coefficient = bf16[16,2,96,128]{3,2,1,0:T(8,128)(2,1)S(1)} all-to-all(bf16[16,2,96,128]{3,2,1,0:T(8,128)(2,1)S(1)} %partials.3), channel_id=1, replica_groups=mesh['freq'=2,'tile'=16] {'tile'}, dimensions={0} | all-to-all | bytes 1572864 | tf_op jit(solution)/shard_map/all_to_all | solution.py:382
  105.9 4.7 %residual.3 = (f32[2,512,128]{2,1,0:T(8,128)}, bf16[16,2,96,128]{3,2,1,0:T(8,128)(2,1)S(1)}) custom-call(s32[16,16]{1,0:T(8,128)S(1)} %copy-done.4, bf16[2,512,2,1536]{3,2,1,0:T(2,128)(2,1)S(1)} %copy-done, bf16[16,2,96,128]{3,2,1,0:T(8,128)(2,1)S(1)} %all_to_all.22.coefficient, f32[2,512,128]{2,1,0:T(8,128)S(1)} %copy-done.3), custom_call_target="tpu_custom_call" | custom-call | tf_op jit(solution)/shard_map/residual/pallas_call | solution.py:177
  110.7 23.9 %all_to_all.23.coefficient = bf16[16,2,96,128]{3,2,1,0:T(8,128)(2,1)S(1)} all-to-all(bf16[16,2,96,128]{3,2,1,0:T(8,128)(2,1)S(1)} %get-tuple-element.12), channel_id=1, replica_groups=mesh['freq'=2,'tile'=16] {'tile'}, dimensions={0} | all-to-all | bytes 1572864 | tf_op jit(solution)/shard_map/all_to_all | solution.py:382
  134.5 1.1 update.9.rest_0_
  135.7 0.5 collective-permute-start.3
  136.2 0.7 update.10.rest_0_
  136.9 1.6 %collective-permute-start.4 = (bf16[2,128,128]{2,1,0:T(8,128)(2,1)S(1)}, bf16[2,128,128]{2,1,0:T(8,128)(2,1)S(1)}, u32[]{:S(2)}, u32[]{:S(2)}) collective-permute-start(bf16[2,128,128]{2,1,0:T(8,128)(2,1)S(1)} %update.10.rest_0_), channel_id=1, source_target_pairs={{16,0},{0,16},{17,1},{1,17},{18,2},{2,18},{19,3},{3,19},{20,4},{4,... | collective-permute-start | bytes 196616 | tf_op jit(solution)/shard_map/ppermute | solution.py:395
  138.5 0.7 update.11.rest_0_
  139.2 0.5 collective-permute-start.5
  139.7 3.8 %collective-permute-done.4.rest_1_ = bf16[2,128,128]{2,1,0:T(8,128)(2,1)S(1)} collective-permute-done((bf16[2,128,128]{2,1,0:T(8,128)(2,1)S(1)}, bf16[2,128,128]{2,1,0:T(8,128)(2,1)S(1)}, u32[]{:S(2)}, u32[]{:S(2)}) %collective-permute-start.4) | collective-permute-done | bytes 65568 | tf_op jit(solution)/shard_map/ppermute | solution.py:395
  143.5 2.7 %sparsify.9.rest_2_ = f32[2,128,128]{2,1,0:T(8,128)S(1)} custom-call(s32[256,128]{1,0:T(8,128)S(1)} %get-tuple-element.8.mute, f32[1,128]{1,0:T(1,128)S(1)} %get-tuple-element.9.cutoff, bf16[256,8]{1,0:T(8,128)(2,1)S(1)} %get-tuple-element.10.ahead, bf16[8,256]{1,0:T(8,128)(2,1)S(1)} %get-tuple-element.11.back, bf16[2,128,128]{2,1,0:T(8,128)(2,1)S(1)} %update.10.rest_0_, ...), custom_call_target="tpu_custom_call" | custom-call | tf_op jit(solution)/shard_map/sparsify/pallas_call | solution.py:325
  146.2 2.7 %sparsify.10.rest_3_ = f32[2,128,128]{2,1,0:T(8,128)S(1)} custom-call(s32[256,128]{1,0:T(8,128)S(1)} %get-tuple-element.8.mute, f32[1,128]{1,0:T(1,128)S(1)} %get-tuple-element.9.cutoff, bf16[256,8]{1,0:T(8,128)(2,1)S(1)} %get-tuple-element.10.ahead, bf16[8,256]{1,0:T(8,128)(2,1)S(1)} %get-tuple-element.11.back, bf16[2,128,128]{2,1,0:T(8,128)(2,1)S(1)} %update.11.rest_0_, ...), custom_call_target="tpu_custom_call" | custom-call | tf_op jit(solution)/shard_map/sparsify/pallas_call | solution.py:325
  148.9 5.9 %sparsify.11 = f32[2,512,128]{2,1,0:T(8,128)} custom-call(s32[256,128]{1,0:T(8,128)S(1)} %get-tuple-element.8.mute, f32[1,128]{1,0:T(1,128)S(1)} %get-tuple-element.9.cutoff, bf16[256,8]{1,0:T(8,128)(2,1)S(1)} %get-tuple-element.10.ahead, bf16[8,256]{1,0:T(8,128)(2,1)S(1)} %get-tuple-element.11.back, bf16[2,256,128]{2,1,0:T(8,128)(2,1)S(1)} %update.9.rest_0_, ...), custom_call_target="tpu_custom_call" | custom-call | tf_op jit(solution)/shard_map/sparsify/pallas_call | solution.py:325
  (20 shorter events, 0.0 us)
Async XLA Ops:
  0.6 32.9 %copy-start.4 = (s32[16,16]{1,0:T(8,128)S(1)}, s32[16,16]{1,0:T(8,128)}, u32[]{:S(2)}) copy-start(s32[16,16]{1,0:T(8,128)} %ranks.5) | copy-start | bytes 3076
  0.6 32.9 %copy-start.3 = (f32[2,512,128]{2,1,0:T(8,128)S(1)}, f32[2,512,128]{2,1,0:T(8,128)}, u32[]{:S(2)}) copy-start(f32[2,512,128]{2,1,0:T(8,128)} %recorded.3) | copy-start | bytes 1572868
  0.6 32.9 %copy-start = (bf16[2,512,2,1536]{3,2,1,0:T(2,128)(2,1)S(1)}, bf16[2,512,2,1536]{3,2,1,0:T(2,128)(2,1)}, u32[]{:S(2)}) copy-start(bf16[2,512,2,1536]{3,2,1,0:T(2,128)(2,1)} %basis.14) | copy-start | bytes 18874372
  5.7 55.9 %slice-start = ((s8[6291456]{0:T(1024)(128)(4,1)}), s8[4194304]{0:T(1024)(128)(4,1)S(1)}, s32[]{:S(2)}) async-start(s8[6291456]{0:T(1024)(128)(4,1)} %bitcast.2), calls=%async_computation.4 | async-start | bytes 8388608
  5.7 55.9 %copy-start.1 = (f32[2,512,128]{2,1,0:T(8,128)S(1)}, f32[2,512,128]{2,1,0:T(8,128)}, u32[]{:S(2)}) copy-start(f32[2,512,128]{2,1,0:T(8,128)} %model.5) | copy-start | bytes 1572868
  33.5 28.1 %slice-start.1 = ((s8[6291456]{0:T(1024)(128)(4,1)}), s8[2097152]{0:T(1024)(128)(4,1)S(1)}, s32[]{:S(2)}) async-start(s8[6291456]{0:T(1024)(128)(4,1)} %bitcast.2), calls=%async_computation.5 | async-start | bytes 4194304
  62.3 5.6 %copy-start.2 = (bf16[16,2,96,128]{3,2,1,0:T(8,128)(2,1)S(1)}, bf16[16,2,96,128]{3,2,1,0:T(8,128)(2,1)}, u32[]{:S(2)}) copy-start(bf16[16,2,96,128]{3,2,1,0:T(8,128)(2,1)} %partials.2._) | copy-start | bytes 2359300
  62.3 5.6 %copy-start.5 = (s32[512,64]{0,1:T(8,128)S(1)}, s32[512,64]{0,1:T(8,128)}, u32[]{:S(2)}) copy-start(s32[512,64]{0,1:T(8,128)} %param.12) | copy-start | bytes 393220
  62.3 5.5 %copy-start.6 = (f32[64]{0:T(128)S(1)}, f32[64]{0:T(128)}, u32[]{:S(2)}) copy-start(f32[64]{0:T(128)} %param.13) | copy-start | bytes 772
  62.3 9.6 %collective-permute-start = (bf16[2,128,128]{2,1,0:T(8,128)(2,1)S(1)}, bf16[2,128,128]{2,1,0:T(8,128)(2,1)S(1)}, u32[]{:S(2)}, u32[]{:S(2)}) collective-permute-start(bf16[2,128,128]{2,1,0:T(8,128)(2,1)S(1)} %update.6.rest_0_), channel_id=1, source_target_pairs={{16,0},{0,16},{17,1},{1,17},{18,2},{2,18},{19,3},{3,19},{20,4},{4,... | collective-permute-start | bytes 196616 | tf_op jit(solution)/shard_map/ppermute | solution.py:395
  64.5 4.7 %collective-permute-start.1 = (bf16[2,128,128]{2,1,0:T(8,128)(2,1)S(1)}, bf16[2,128,128]{2,1,0:T(8,128)(2,1)S(1)}, u32[]{:S(2)}, u32[]{:S(2)}) collective-permute-start(bf16[2,128,128]{2,1,0:T(8,128)(2,1)S(1)} %update.7.rest_0_), channel_id=1, source_target_pairs={{16,0},{0,16},{17,1},{1,17},{18,2},{2,18},{19,3},{3,19},{20,4},{4,... | collective-permute-start | bytes 196616 | tf_op jit(solution)/shard_map/ppermute | solution.py:395
  66.3 8.3 %collective-permute-start.2 = (bf16[2,256,128]{2,1,0:T(8,128)(2,1)S(1)}, bf16[2,256,128]{2,1,0:T(8,128)(2,1)S(1)}, u32[]{:S(2)}, u32[]{:S(2)}) collective-permute-start(bf16[2,256,128]{2,1,0:T(8,128)(2,1)S(1)} %update.8.rest_0_), channel_id=1, source_target_pairs={{16,0},{0,16},{17,1},{1,17},{18,2},{2,18},{19,3},{3,19},{20,4},{4,... | collective-permute-start | bytes 393224 | tf_op jit(solution)/shard_map/ppermute | solution.py:395
  135.7 13.2 %collective-permute-start.3 = (bf16[2,256,128]{2,1,0:T(8,128)(2,1)S(1)}, bf16[2,256,128]{2,1,0:T(8,128)(2,1)S(1)}, u32[]{:S(2)}, u32[]{:S(2)}) collective-permute-start(bf16[2,256,128]{2,1,0:T(8,128)(2,1)S(1)} %update.9.rest_0_), channel_id=1, source_target_pairs={{16,0},{0,16},{17,1},{1,17},{18,2},{2,18},{19,3},{3,19},{20,4},{4,... | collective-permute-start | bytes 393224 | tf_op jit(solution)/shard_map/ppermute | solution.py:395
  136.9 6.6 %collective-permute-start.4 = (bf16[2,128,128]{2,1,0:T(8,128)(2,1)S(1)}, bf16[2,128,128]{2,1,0:T(8,128)(2,1)S(1)}, u32[]{:S(2)}, u32[]{:S(2)}) collective-permute-start(bf16[2,128,128]{2,1,0:T(8,128)(2,1)S(1)} %update.10.rest_0_), channel_id=1, source_target_pairs={{16,0},{0,16},{17,1},{1,17},{18,2},{2,18},{19,3},{3,19},{20,4},{4,... | collective-permute-start | bytes 196616 | tf_op jit(solution)/shard_map/ppermute | solution.py:395
  139.2 7.0 %collective-permute-start.5 = (bf16[2,128,128]{2,1,0:T(8,128)(2,1)S(1)}, bf16[2,128,128]{2,1,0:T(8,128)(2,1)S(1)}, u32[]{:S(2)}, u32[]{:S(2)}) collective-permute-start(bf16[2,128,128]{2,1,0:T(8,128)(2,1)S(1)} %update.11.rest_0_), channel_id=1, source_target_pairs={{16,0},{0,16},{17,1},{1,17},{18,2},{2,18},{19,3},{3,19},{20,4},{4,... | collective-permute-start | bytes 196616 | tf_op jit(solution)/shard_map/ppermute | solution.py:395
